TPU v7x, 256 devices: a whole 4x4x8 slice. The times are simulated.
256 devices in a mesh: cable: 4 (over y), fx: 32 (over z, x), fz: 2 (over core).
Axes of the slice: x: 4, y: 4, z: 8, core: 2. Of those that a mesh axis runs over, the one named last changes fastest.
Arguments:
- velocity: float32 [3, 256, 64, 256], P(None, 'fx', 'cable', 'fz'), may hold values from -6 to 6
- viscosity: float32 [256, 64, 256], P('fx', 'cable', 'fz'), may hold values from 0.02 to 0.15
- disp_init: float32 [3, 16384], P(None, ('cable', 'fx', 'fz')), may hold values from -3 to 3
- rest_shape: float32 [3, 16384], P(None, ('cable', 'fx', 'fz')), may hold values from -6 to 6
- compliance: float32 [16384], P(('cable', 'fx', 'fz')), may hold values from 0.5 to 2
- stencil_weights: float32 [3, 12, 16384], P(None, None, ('cable', 'fx', 'fz')), may hold values from 0.05 to 0.45
- anchor: int32 [3, 16384], P(None, ('cable', 'fx', 'fz')), may hold values from 0 to 9852, as said below
- owners: int32 [3, 16384], P(None, ('cable', 'fx', 'fz')), may hold values from 0 to 63, as said below
Outputs:
- disp_next: float32 [3, 16384], P(None, ('cable', 'fx', 'fz'))
- velocity_out: float32 [3, 256, 64, 256], P(None, 'fx', 'cable', 'fz')
Inputs may be any that keep to these rules, and one draw needn't show every extreme that they name: `owners`: the owner's number is fx * 2 + fz of a fluid block in the segment's own cable group. Among the 64 segments of one device (aligned blocks of 64 segments), at most 4 name the same owner in one iteration; in every iteration one owner is named by exactly 4 segments of every device of each group. `anchor`: the cell is numbered (x * 16 + y) * 128 + z in the owner's block, with x <= 4, y <= 12 and z <= 124, so the 4 x 4 x 4 stencil lies inside that block.
All inputs are finite; a program needn't handle non-finite values.
Results may differ from a plain program's by a relative error of at most 0.0003.
Values sent between devices are 32-bit elements; how exact they have to be, the bound alone decides.
No kernel may reach another device: no remote copies, remote signals or barrier semaphores. Data moves between devices by JAX's collectives and lax.ppermute only.
A program may use at most 64 MiB of HBM per device.

v0:
```python
import jax
import jax.numpy as jnp
from jax import lax
from jax.sharding import PartitionSpec as P

ITERS = 3


spread_gain = 16.0
drag_coeff = 0.05
relaxation = 0.5
ridge_share = 0.01


def with_halo(cells, sides, width):
    for axis, dim in sides:
        count = lax.axis_size(axis)
        ends = count - 1
        head = lax.slice_in_dim(cells, 0, width, axis=dim)
        tail = lax.slice_in_dim(cells, cells.shape[dim] - width, cells.shape[dim], axis=dim)
        cells = jnp.concatenate(
            [
                lax.ppermute(tail, axis, [(i, (i + 1) % count) for i in range(ends)]),
                cells,
                lax.ppermute(head, axis, [((i + 1) % count, i) for i in range(ends)]),
            ],
            axis=dim,
        )
    return cells


def stencil_table(weights):
    table = (
        weights[0:4][:, None, None, :]
        * weights[4:8][None, :, None, :]
        * weights[8:12][None, None, :, :]
    )
    return table.reshape(64, weights.shape[1])


def face_sum(padded):
    beside = padded[:, 2:, 1:-1, 1:-1] + padded[:, :-2, 1:-1, 1:-1]
    beside = beside + padded[:, 1:-1, 2:, 1:-1] + padded[:, 1:-1, :-2, 1:-1]
    beside = beside + padded[:, 1:-1, 1:-1, 2:] + padded[:, 1:-1, 1:-1, :-2]
    return beside


def solve_small(gram, width):
    square = gram[:width, :width]
    target = gram[:width, width]
    shift = ridge_share * jnp.trace(square) / width + 1e-06
    if width == 1:
        return [-target[0] / (square[0, 0] + shift)]
    first = square[0, 0] + shift
    second = square[1, 1] + shift
    cross = square[0, 1]
    determinant = first * second - cross * cross
    return [
        -(second * target[0] - cross * target[1]) / determinant,
        -(first * target[1] - cross * target[0]) / determinant,
    ]


def body(velocity, viscosity, disp_init, rest_shape, compliance, stencil_weights, anchor, owners):
    member = lax.axis_index(("fx", "fz"))
    seg_count = disp_init.shape[1]
    seg_total = seg_count * lax.axis_size(("cable", "fx", "fz"))
    position = lax.axis_index(("cable", "fx", "fz")) * seg_count + jnp.arange(
        seg_count, dtype=jnp.int32
    )
    tension_ramp = 1.0 + 2.0 * position.astype(jnp.float32) / seg_total
    size_x, size_y, size_z = viscosity.shape
    cells = size_x * size_y * size_z
    slot_total = 4 * seg_count
    steps_one = jnp.arange(4, dtype=jnp.int32)
    offsets = (
        (steps_one[:, None, None] * size_y + steps_one[None, :, None]) * size_z
        + steps_one[None, None, :]
    ).reshape(64)
    current = disp_init
    residuals = []
    responses = []
    velocity_out = velocity
    for iteration in range(ITERS):
        corner_row = anchor[iteration].astype(jnp.float32)[None]
        payload = jnp.concatenate([current, stencil_weights[iteration], corner_row], axis=0)
        owner_row = owners[iteration].astype(jnp.float32)[None]
        everyone = lax.all_gather(
            jnp.concatenate([payload, owner_row], axis=0), ("fx", "fz"), axis=1, tiled=True
        )
        owned = (everyone[16].astype(jnp.int32) == member).astype(jnp.int32)
        rank = jnp.cumsum(owned) - owned
        slot_place = jnp.where(owned > 0, rank, slot_total)
        compact = (
            jnp.zeros((16, slot_total + 1), jnp.float32)
            .at[:, slot_place]
            .set(everyone[0:16])[:, :slot_total]
        )
        corner = compact[15].astype(jnp.int32)
        cell_index = corner[None, :] + offsets[:, None]
        stencil = stencil_table(compact[3:15])
        spread_terms = spread_gain * stencil[None] * compact[0:3][:, None, :]
        forcing = (
            jnp.zeros((3, cells), jnp.float32)
            .at[:, cell_index.reshape(-1)]
            .add(spread_terms.reshape(3, -1))
        )
        forcing_field = forcing.reshape(velocity.shape)
        u_star = velocity + forcing_field
        padded = with_halo(u_star, (("cable", 2), ("fx", 1), ("fz", 3)), 1)
        beside = face_sum(padded)
        laplace = beside - 6.0 * u_star
        speed = jnp.sqrt(1.0 + jnp.sum(u_star * u_star, axis=0, keepdims=True))
        u_new = u_star + viscosity[None] * laplace - drag_coeff * u_star * speed
        picked = u_new.reshape(3, cells)[:, cell_index]
        sampled = jnp.sum(stencil[None] * picked, axis=1)
        widened = jnp.concatenate([sampled, jnp.zeros((3, 1), jnp.float32)], axis=1)
        spread_back = widened[:, slot_place]
        returned = lax.psum_scatter(spread_back, ("fx", "fz"), scatter_dimension=1, tiled=True)
        response = rest_shape + compliance[None] * tension_ramp[None] * returned
        response, velocity_out = (response, u_new)
        residual = response - current
        if iteration == 0:
            following = current + relaxation * residual
        else:
            columns = [residual - earlier for earlier in residuals]
            changes = [response - earlier for earlier in responses]
            matrix = jnp.stack(columns + [residual]).reshape(iteration + 1, -1)
            partial_gram = jnp.dot(matrix, matrix.T, precision=lax.Precision.HIGHEST)
            gram = lax.psum(partial_gram, ("cable", "fx", "fz"))
            coefs = solve_small(gram, iteration)
            following = response
            for column in range(iteration):
                following = following + coefs[column] * changes[column]
        residuals.append(residual)
        responses.append(response)
        current = following
    return (current, velocity_out)


def solution(mesh):
    placed = (
        P(None, "fx", "cable", "fz"),
        P("fx", "cable", "fz"),
        P(None, ("cable", "fx", "fz")),
        P(None, ("cable", "fx", "fz")),
        P(("cable", "fx", "fz")),
        P(None, None, ("cable", "fx", "fz")),
        P(None, ("cable", "fx", "fz")),
        P(None, ("cable", "fx", "fz")),
    )
    return jax.shard_map(
        body,
        mesh=mesh,
        in_specs=placed,
        out_specs=(P(None, ("cable", "fx", "fz")), P(None, "fx", "cable", "fz")),
        check_vma=False,
    )
```

profile of v0, /device:TPU:1, one launch (start us, length us, event | category | flops | bytes accessed | tf_op | source)
XLA Modules:
  0.0 1474.1 jit_solution(890402977995218385)
XLA Ops:
  9.5 55.1 %all-gather = f32[64,64,17]{1,2,0:T(8,128)S(1)} all-gather(f32[1,64,17]{1,2,0:T(8,128)S(1)} %maximum_bitcast_fusion), channel_id=1, replica_groups=mesh['cable'=4,'fx'=32,'fz'=2] {'fx','fz'}, dimensions={0}, use_global_device_ids=true | all-gather | bytes 282880 | tf_op jit(solution)/shard_map/all_gather | solution.py:88
  66.2 10.6 scatter_custom_fusion
  78.0 4.6 bitcast_multiply_fusion.2
  82.6 108.6 %scatter_custom_fusion.1 = f32[3,16384]{0,1:T(8,128)} fusion(s32[16384]{0:T(1024)S(1)} %bitcast.195, f32[3,16384]{0,1:T(8,128)} %bitcast_multiply_fusion.2, f32[]{:T(128)} %constant.30.clone.1), kind=kCustom, calls=%fused_computation.18 | custom fusion | flops 49152 | bytes 393220 | tf_op jit(solution)/shard_map/scatter-add | solution.py:106
  191.2 5.3 copy.63
  196.5 3.6 collective-permute-start
  201.6 3.0 collective-permute-done.1
  204.6 2.6 collective-permute-start.3
  208.5 3.4 collective-permute-done.2
  212.1 4.8 collective-permute-start.4
  218.5 2.0 collective-permute-done.5
  220.8 4.6 copy.64
  225.5 57.8 %gather_fusion = f32[16384,3]{1,0:T(8,128)} fusion(f32[3,16384]{0,1:T(8,128)} %bitcast.156, s32[16384]{0:T(1024)S(1)} %broadcast_clamp_fusion.2), kind=kCustom, calls=%fused_computation | custom fusion | bytes 458752 | tf_op jit(solution)/shard_map/gather | solution.py:115
  283.3 5.3 multiply_reduce_fusion.2
  288.6 14.1 gather_fusion.1
  302.8 137.3 %reduce-scatter.10.cloned.1.call-done = f32[64,3]{1,0:T(8,128)} async-done(((f32[4096,3]{1,0:T(8,128)}), f32[64,3]{1,0:T(8,128)}) %reduce-scatter.10.cloned.1.call-update) | async-done | bytes 784
  441.0 55.1 %all-gather.1 = f32[64,64,17]{1,2,0:T(8,128)S(1)} all-gather(f32[1,64,17]{1,2,0:T(8,128)S(1)} %maximum_bitcast_fusion.1), channel_id=1, replica_groups=mesh['cable'=4,'fx'=32,'fz'=2] {'fx','fz'}, dimensions={0}, use_global_device_ids=true | all-gather | bytes 282880 | tf_op jit(solution)/shard_map/all_gather | solution.py:88
  497.6 10.6 scatter_custom_fusion.2
  509.4 4.6 bitcast_multiply_fusion.1
  513.9 108.7 %scatter_custom_fusion.3 = f32[3,16384]{0,1:T(8,128)} fusion(s32[16384]{0:T(1024)S(1)} %bitcast.196, f32[3,16384]{0,1:T(8,128)} %bitcast_multiply_fusion.1, f32[]{:T(128)} %constant.30.clone.1), kind=kCustom, calls=%fused_computation.15 | custom fusion | flops 49152 | bytes 393220 | tf_op jit(solution)/shard_map/scatter-add | solution.py:106
  622.6 5.2 copy.71
  627.9 3.3 collective-permute-start.6
  632.5 3.1 collective-permute-done.7
  635.7 2.2 collective-permute-start.9
  639.2 3.4 collective-permute-done.8
  642.8 4.8 collective-permute-start.10
  651.5 4.6 copy.72
  656.1 57.8 %gather_fusion.2 = f32[16384,3]{1,0:T(8,128)} fusion(f32[3,16384]{0,1:T(8,128)} %bitcast.157, s32[16384]{0:T(1024)S(1)} %broadcast_clamp_fusion.1), kind=kCustom, calls=%fused_computation.2 | custom fusion | bytes 458752 | tf_op jit(solution)/shard_map/gather | solution.py:115
  713.9 5.3 multiply_reduce_fusion.1
  719.2 14.1 gather_fusion.3
  733.4 137.9 %reduce-scatter.12.cloned.1.call-done = f32[64,3]{1,0:T(8,128)} async-done(((f32[4096,3]{1,0:T(8,128)}), f32[64,3]{1,0:T(8,128)}) %reduce-scatter.12.cloned.1.call-update) | async-done | bytes 784
  872.2 79.6 %psum.14 = f32[2,2]{1,0:T(2,128)S(1)} all-reduce(f32[2,2]{1,0:T(2,128)S(1)} %convolution_bitcast_fusion.1), channel_id=1, replica_groups=mesh['cable'=4,'fx'=32,'fz'=2] {'cable','fx','fz'}, use_global_device_ids=true, to_apply=%region_14.15 | all-reduce | flops 4 | bytes 32 | tf_op jit(solution)/shard_map/psum | solution.py:130
  954.4 50.5 %all-gather.2 = f32[64,64,17]{1,2,0:T(8,128)S(1)} all-gather(f32[1,64,17]{1,2,0:T(8,128)S(1)} %maximum_bitcast_fusion.2), channel_id=1, replica_groups=mesh['cable'=4,'fx'=32,'fz'=2] {'fx','fz'}, dimensions={0}, use_global_device_ids=true | all-gather | bytes 282880 | tf_op jit(solution)/shard_map/all_gather | solution.py:88
  1006.6 10.6 scatter_custom_fusion.4
  1018.3 4.6 bitcast_multiply_fusion
  1022.9 108.8 %scatter_custom_fusion.5 = f32[3,16384]{0,1:T(8,128)} fusion(s32[16384]{0:T(1024)S(1)} %bitcast.197, f32[3,16384]{0,1:T(8,128)} %bitcast_multiply_fusion, f32[]{:T(128)} %constant.30.clone.1), kind=kCustom, calls=%fused_computation.12 | custom fusion | flops 49152 | bytes 393220 | tf_op jit(solution)/shard_map/scatter-add | solution.py:106
  1131.7 5.2 copy.80
  1139.6 3.1 collective-permute-done.13
  1142.8 3.0 collective-permute-start.15
  1147.1 3.4 collective-permute-done.14
  1150.7 4.9 collective-permute-start.16
  1157.0 2.2 collective-permute-done.17
  1159.6 4.6 copy.81
  1164.2 57.8 %gather_fusion.4 = f32[16384,3]{1,0:T(8,128)} fusion(f32[3,16384]{0,1:T(8,128)} %bitcast.158, s32[16384]{0:T(1024)S(1)} %broadcast_clamp_fusion), kind=kCustom, calls=%fused_computation.4 | custom fusion | bytes 458752 | tf_op jit(solution)/shard_map/gather | solution.py:115
  1222.0 5.2 multiply_reduce_fusion
  1227.3 14.1 gather_fusion.5
  1241.4 136.3 %reduce-scatter.14.cloned.1.call-done = f32[64,3]{1,0:T(8,128)} async-done(((f32[4096,3]{1,0:T(8,128)}), f32[64,3]{1,0:T(8,128)}) %reduce-scatter.14.cloned.1.call-update) | async-done | bytes 784
  1378.7 79.6 %psum.15 = f32[3,3]{1,0:T(4,128)S(1)} all-reduce(f32[3,3]{1,0:T(4,128)S(1)} %convolution_bitcast_fusion), channel_id=1, replica_groups=mesh['cable'=4,'fx'=32,'fz'=2] {'cable','fx','fz'}, use_global_device_ids=true, to_apply=%region_22.23 | all-reduce | flops 9 | bytes 72 | tf_op jit(solution)/shard_map/psum | solution.py:130
  (173 shorter events, 33.2 us)
Async XLA Ops:
  7.2 432.9 %reduce-scatter.10.cloned.1.call-start = ((), (), s32[]{:S(2)}) async-start(), calls=%async_computation.3 | async-start | bytes 2129920
  191.2 5.3 copy-start
  191.2 29.4 %copy-start.2 = (f32[8,16,128]{2,1,0:T(8,128)S(1)}, f32[8,16,128]{2,1,0:T(8,128)}, u32[]{:S(2)}) copy-start(f32[8,16,128]{2,1,0:T(8,128)} %param.9) | copy-start | bytes 196612
  196.5 5.1 collective-permute-start
  200.1 4.4 collective-permute-start.1
  204.6 3.9 collective-permute-start.3
  207.2 4.7 collective-permute-start.2
  212.1 6.4 collective-permute-start.4
  216.9 3.6 collective-permute-start.5
  225.5 77.3 %copy-start.5 = (f32[64]{0:T(128)S(1)}, f32[64]{0:T(128)}, u32[]{:S(2)}) copy-start(f32[64]{0:T(128)} %param.12) | copy-start | bytes 772
  225.5 215.4 %copy-start.3 = (f32[3,64]{1,0:T(4,128)S(1)}, f32[3,64]{1,0:T(4,128)}, u32[]{:S(2)}) copy-start(f32[3,64]{1,0:T(4,128)} %param.11) | copy-start | bytes 2308
  225.5 215.4 %copy-start.4 = (f32[3,64]{1,0:T(4,128)S(1)}, f32[3,64]{1,0:T(4,128)}, u32[]{:S(2)}) copy-start(f32[3,64]{1,0:T(4,128)} %param.10) | copy-start | bytes 2308
  302.7 568.6 %reduce-scatter.12.cloned.1.call-start = ((), (), s32[]{:S(2)}) async-start(), calls=%async_computation.4 | async-start | bytes 2129920
  627.9 4.6 collective-permute-start.6
  631.2 4.4 collective-permute-start.7
  635.7 3.5 collective-permute-start.9
  637.8 4.7 collective-permute-start.8
  642.8 6.4 collective-permute-start.10
  647.6 3.6 collective-permute-start.11
  733.3 644.4 %reduce-scatter.14.cloned.1.call-start = ((), (), s32[]{:S(2)}) async-start(), calls=%async_computation.5 | async-start | bytes 2129920
  1137.0 2.6 collective-permute-start.12
  1138.3 4.4 collective-permute-start.13
  1142.8 4.3 collective-permute-start.15
  1145.8 4.7 collective-permute-start.14
  1150.7 6.3 collective-permute-start.16
  1155.7 3.6 collective-permute-start.17
  1159.6 67.7 %copy-start.1 = (f32[3,8,16,128]{3,2,1,0:T(8,128)}, f32[3,8,16,128]{3,2,1,0:T(8,128)S(1)}, u32[]{:S(2)}) copy-start(f32[3,8,16,128]{3,2,1,0:T(8,128)S(1)} %fusion.13) | copy-start | bytes 589828
Sparse Core Ops, SparseCore 0:
  302.8 137.2 reduce-scatter.9
  733.4 137.7 reduce-scatter.11
  1241.5 136.1 reduce-scatter.13
where the time goes:
time: 1480 us; the launch traced here: 1470 us
  waiting for transfers between devices  437 us (30%)
  other arithmetic  363 us (25%)
  blocking collectives  320 us (22%)
  local copies, waits for them, and re-layouts  287 us (19%)
  starting transfers between devices  42.6 us (3%)
  between operations  24.1 us (2%)
    unnamed x6, waiting for transfers between devices  412 us
    scatter-add x3, other arithmetic, body(): forcing = jnp.zeros((3, cells), jnp.float32).at[:, cell_index.reshape(-1)...  326 us
    gather x3, local copies, waits for them, and re-layouts, body(): picked = u_new.reshape(3, cells)[:, cell_index]  173 us
    all_gather x3, blocking collectives, body(): lax.all_gather(jnp.concatenate([payload, owner_row], axis=0), ('fx', 'fz'...  161 us
    psum x2, blocking collectives, body(): gram = lax.psum(partial_gram, ('cable', 'fx', 'fz'))  159 us
    gather x3, local copies, waits for them, and re-layouts, body(): spread_back = widened[:, slot_place]  42.3 us
    scatter x3, local copies, waits for them, and re-layouts, body(): compact = jnp.zeros((16, slot_total + 1), jnp.float32).at[:, slot_place]....  31.9 us
  transfers between devices with their start and end apart: 21, of which 12 were waited for; matrix products, arithmetic and copies ran while one was open for 0% of the time, Pallas kernels for 0%

commit v1 on v0

v1 whole, which is shorter than its diff:
```python
import functools

import jax
import jax.numpy as jnp
from jax import lax
from jax.experimental import pallas as pl
from jax.experimental.pallas import tpu as pltpu
from jax.sharding import PartitionSpec as P

F32 = jnp.float32
BF16 = jnp.bfloat16
NT = (((1,), (1,)), ((), ()))
NN = (((1,), (0,)), ((), ()))
EXACT = lax.Precision.HIGHEST

spread_gain = 16.0
drag_coeff = 0.05
relaxation = 0.5
ridge_share = 0.01

SEG_DEV = 64
GROUP = 64
CAP = 4
SLOTS = GROUP * CAP
SX, SY, SZ = 8, 16, 128
XY = SX * SY

R_W, R_A, R_D0, R_REST, R_CR, R_CODE = 0, 12, 15, 18, 21, 22


def split(x):
    hi = x.astype(BF16)
    return hi, (x - hi.astype(F32)).astype(BF16)


def dot3(a, b, dims):
    f = functools.partial(lax.dot_general, dimension_numbers=dims, preferred_element_type=F32)
    return f(a[0], b[0]) + (f(a[0], b[1]) + f(a[1], b[0]))


def iota(shape, dim):
    return lax.broadcasted_iota(jnp.int32, shape, dim)


def pack_kernel(disp, rest, comp, weights, anchor, owner, msg, place, fields):
    fz_n, fx_n, cable_n = lax.axis_size("fz"), lax.axis_size("fx"), lax.axis_size("cable")
    device = (lax.axis_index("cable") * fx_n + lax.axis_index("fx")) * fz_n + lax.axis_index("fz")
    position = (device * SEG_DEV + iota((1, SEG_DEV), 1)).astype(F32)
    ramp = 1.0 + 2.0 * position / (SEG_DEV * fz_n * fx_n * cable_n)
    dest = iota((GROUP, SEG_DEV), 0)
    earlier = (iota((SEG_DEV, SEG_DEV), 0) < iota((SEG_DEV, SEG_DEV), 1)).astype(F32)
    hots, ranks, codes = [], [], []
    for t in range(3):
        own = owner[t : t + 1, :]
        hot = (dest == own).astype(F32)
        before = lax.dot_general(hot, earlier, NN, preferred_element_type=F32)
        rank = jnp.sum(hot * before, axis=0, keepdims=True)
        hots.append(hot)
        ranks.append(rank)
        codes.append(own.astype(F32) * CAP + rank)
    fields[...] = jnp.zeros_like(fields)
    fields[R_D0 : R_D0 + 3, :] = disp[...]
    fields[R_REST : R_REST + 3, :] = rest[...]
    fields[R_CR : R_CR + 1, :] = comp[...] * ramp
    fields[R_CODE : R_CODE + 1, :] = codes[0]
    fields[R_CODE + 1 : R_CODE + 2, :] = codes[1]
    for t in range(3):
        cell = anchor[t : t + 1, :]
        fields[R_W : R_W + 12, :] = weights[t]
        fields[R_A : R_A + 1, :] = (cell >> 11).astype(F32)
        fields[R_A + 1 : R_A + 2, :] = ((cell >> 7) & (SY - 1)).astype(F32)
        fields[R_A + 2 : R_A + 3, :] = (cell & (SZ - 1)).astype(F32)
        now = fields[...]
        placed = jnp.concatenate([jnp.where(ranks[t] == k, now, 0.0) for k in range(CAP)], axis=0)
        msg[:, 128 * t : 128 * t + 128] = lax.dot_general(
            hots[t], placed, NT, precision=EXACT, preferred_element_type=F32
        )
    place[...] = jnp.zeros_like(place)
    place[0:1, :] = owner[2:3, :].astype(F32)
    place[1:2, :] = ranks[2]


def slot_rows(block):
    wide = jnp.concatenate([block, jnp.zeros((128 - GROUP, 128), F32)], axis=0)
    turned = jnp.transpose(wide)
    low = turned[0:32] + pltpu.roll(turned[32:64], 64, 1)
    high = turned[64:96] + pltpu.roll(turned[96:128], 64, 1)
    return jnp.concatenate([low, high], axis=1)


def along(rows, first, start, extent):
    at = iota((extent, SLOTS), 0).astype(F32) - rows[start : start + 1]
    total = jnp.zeros((extent, SLOTS), F32)
    for i in range(4):
        total = jnp.where(at == i, rows[first + i : first + i + 1], total)
    return total


def tables(rows):
    wx = along(rows, R_W, R_A, SX)
    wy = along(rows, R_W + 4, R_A + 1, SY)
    wz = along(rows, R_W + 8, R_A + 2, SZ)
    wxy = jnp.concatenate([wx[x : x + 1] * wy for x in range(SX)], axis=0)
    return wxy, wz


def spread(wxy2, wz, disp):
    return dot3(wxy2, split(wz * (spread_gain * disp)), NT)


def look_up(sent, code):
    low_half = iota((1, 128), 1) < 64
    label = (iota((GROUP, SLOTS), 0) * CAP + iota((GROUP, SLOTS), 1) // 64).astype(F32)
    halves = [[None] * 2 for _ in range(3)]
    for half in range(2):
        piece = code[:, 128 * half : 128 * half + 128]
        turned = pltpu.roll(piece, 64, 1)
        found = []
        for odd in range(2):
            both = jnp.where(low_half, turned, piece) if odd else jnp.where(low_half, piece, turned)
            match = label == jnp.concatenate([both, both], axis=1)
            per = []
            for comp in range(3):
                hit = jnp.where(match, sent[:, comp * SLOTS : (comp + 1) * SLOTS], 0.0)
                hit = jnp.sum(hit, axis=0, keepdims=True)
                hit = hit[:, :128] + hit[:, 128:]
                per.append(hit + pltpu.roll(hit, 64, 1))
            found.append(per)
        for comp in range(3):
            halves[comp][half] = jnp.where(low_half, found[0][comp], found[1][comp])
    return [jnp.concatenate(halves[comp], axis=1) for comp in range(3)]


def responses(rows, sampled):
    cr = rows[R_CR : R_CR + 1]
    return [rows[R_REST + c : R_REST + c + 1] + cr * sampled[c] for c in range(3)]


def put_faces(field, first, xlo, xhi, ylo, yhi):
    for c in range(3):
        xlo[first + c] = field[first + c, 0:SY, :]
        xhi[first + c] = field[first + c, XY - SY : XY, :]
        ylo[first + c] = field[first + c, pl.ds(0, SX, stride=SY), :]
        yhi[first + c] = field[first + c, pl.ds(SY - 1, SX, stride=SY), :]


def spread_kernel(t, *refs):
    static, velocity = refs[0:2]
    sent = refs[2 : 2 + t]
    field, xlo, xhi, ylo, yhi, wxy_out, wz_out, aux = refs[2 + t : 10 + t]
    rows = slot_rows(static[:, 128 * t : 128 * t + 128])
    wxy, wz = tables(rows)
    wxy_out[...] = wxy
    wz_out[...] = wz
    wxy2 = split(wxy)
    first = [rows[R_D0 + c : R_D0 + c + 1] for c in range(3)]
    aux[...] = jnp.zeros_like(aux)
    if t == 0:
        bases = [first]
    else:
        before = responses(rows, look_up(sent[0], rows[R_CODE : R_CODE + 1]))
        gap = [before[c] - first[c] for c in range(3)]
        second = [first[c] + relaxation * gap[c] for c in range(3)]
        bases = [second]
        kept = [second, gap]
        if t == 2:
            latest = responses(rows, look_up(sent[1], rows[R_CODE + 1 : R_CODE + 2]))
            change = [latest[c] - before[c] for c in range(3)]
            bases = [latest, change]
            kept = [latest, change, gap, [latest[c] - second[c] for c in range(3)], before]
        for n, group in enumerate(kept):
            for c in range(3):
                aux[3 * n + c : 3 * n + c + 1, :] = group[c]
        aux[16:20, :] = rows[R_REST : R_REST + 4]
    for n, base in enumerate(bases):
        for c in range(3):
            forced = spread(wxy2, wz, base[c])
            field[3 * n + c] = velocity[c] + forced if n == 0 else forced
        put_faces(field, 3 * n, xlo, xhi, ylo, yhi)
    if t == 2:
        gram = refs[10 + t]
        total = jnp.sum(sent[1][:, 3 * SLOTS : 3 * SLOTS + 128], axis=0, keepdims=True)
        total = jnp.broadcast_to(total, (8, 128))
        gram[...] = total
        ylo[6] = total
        yhi[6] = total


def wake(u, beside_z, xl, xu, yl, yu, viscosity):
    lane = iota((XY, SZ), 1)
    y = iota((XY, SZ), 0) % SY
    upper_core = lax.axis_index("fz") > 0
    speed = jnp.sqrt(1.0 + (u[0] * u[0] + u[1] * u[1] + u[2] * u[2]))
    new = []
    for c in range(3):
        here = u[c]
        near = jnp.concatenate([xl[c], here[: XY - SY]], axis=0)
        near = near + jnp.concatenate([here[SY:], xu[c]], axis=0)
        wide_l = jnp.concatenate([jnp.broadcast_to(yl[c][x : x + 1], (SY, SZ)) for x in range(SX)], axis=0)
        wide_u = jnp.concatenate([jnp.broadcast_to(yu[c][x : x + 1], (SY, SZ)) for x in range(SX)], axis=0)
        near = near + jnp.where(y == 0, wide_l, pltpu.roll(here, 1, 0))
        near = near + jnp.where(y == SY - 1, wide_u, pltpu.roll(here, XY - 1, 0))
        left = jnp.where(upper_core, beside_z[c], 0.0)
        right = jnp.where(upper_core, 0.0, beside_z[c])
        near = near + pltpu.roll(jnp.where(lane == SZ - 1, left, here), 1, 1)
        near = near + pltpu.roll(jnp.where(lane == 0, right, here), SZ - 1, 1)
        new.append(here + viscosity * (near - 6.0 * here) - drag_coeff * here * speed)
    return new


def sample(new, wxy, wz):
    wz2 = split(wz)
    return [
        jnp.sum(wxy * dot3(split(new[c]), wz2, NN), axis=0, keepdims=True) for c in range(3)
    ]


def total_of(a, b):
    rows = a[0] * b[0] + a[1] * b[1] + a[2] * b[2]
    return jnp.sum(rows, axis=1, keepdims=True)


def in_lanes(values):
    lane = iota((1, 128), 1)
    row = jnp.zeros((1, 128), F32)
    for n, value in enumerate(values):
        row = jnp.where(lane == n, value, row)
    return row


def lane_of(row, n):
    return jnp.sum(jnp.where(iota(row.shape, 1) == n, row, 0.0), axis=1, keepdims=True)


def sample_kernel(t, *refs):
    viscosity, field, beside_z, xl, xu, yl, yu, wxy, wz, aux = refs[0:10]
    inside = (
        lax.axis_index("fx") > 0,
        lax.axis_index("fx") < lax.axis_size("fx") - 1,
        lax.axis_index("cable") > 0,
        lax.axis_index("cable") < lax.axis_size("cable") - 1,
    )

    def whole(ref):
        if t < 2:
            return [ref[c] for c in range(3)]
        return [ref[c] + coef * ref[3 + c] for c in range(3)]

    if t == 2:
        own, across = refs[10:12]
        gram = own[0:1] + yl[6][0:1] + yu[6][0:1] + across[0:1]
        square, target = lane_of(gram, 0), lane_of(gram, 1)
        coef = -target / (square + (ridge_share * square + 1e-06))
    u = whole(field)
    faces = [
        [jnp.where(ok, face, 0.0) for face in whole(ref)]
        for ok, ref in zip(inside, (xl, xu, yl, yu))
    ]
    new = wake(u, whole(beside_z), *faces, viscosity[...])
    sampled = sample(new, wxy[...], wz[...])
    if t == 0:
        msg = refs[10]
        for c in range(3):
            msg[:, SLOTS * c : SLOTS * (c + 1)] = jnp.broadcast_to(sampled[c], (GROUP, SLOTS))
        return

    def kept(n):
        return [aux[3 * n + c : 3 * n + c + 1, :] for c in range(3)]

    cr = aux[19:20, :]
    response = [aux[16 + c : 17 + c, :] + cr * sampled[c] for c in range(3)]
    if t == 1:
        msg = refs[10]
        disp, gap0 = kept(0), kept(1)
        gap = [response[c] - disp[c] for c in range(3)]
        v0 = [gap[c] - gap0[c] for c in range(3)]
        for c in range(3):
            msg[:, SLOTS * c : SLOTS * (c + 1)] = jnp.broadcast_to(sampled[c], (GROUP, SLOTS))
        row = in_lanes([total_of(v0, v0), total_of(v0, gap)])
        msg[:, 3 * SLOTS : 3 * SLOTS + 128] = jnp.broadcast_to(row, (GROUP, 128))
        return
    out, msg, turn = refs[12:15]
    for c in range(3):
        out[c] = new[c]
    latest, change, gap0, gap1, before = (kept(n) for n in range(5))
    disp = [latest[c] + coef * change[c] for c in range(3)]
    gap = [response[c] - disp[c] for c in range(3)]
    v0 = [gap[c] - gap0[c] for c in range(3)]
    v1 = [gap[c] - gap1[c] for c in range(3)]
    row = in_lanes(
        [total_of(v0, v0), total_of(v0, v1), total_of(v1, v1), total_of(v0, gap), total_of(v1, gap)]
    )
    turn[...] = jnp.zeros_like(turn)
    for n, group in enumerate((response, before, latest)):
        for c in range(3):
            turn[3 * n + c : 3 * n + c + 1, :] = group[c][:, :128]
            turn[32 + 3 * n + c : 33 + 3 * n + c, :] = group[c][:, 128:]
    turned = jnp.transpose(turn[...])
    block = turned[0:64] + pltpu.roll(turned[64:128], 16, 1)
    block = block + pltpu.roll(jnp.broadcast_to(row, (8, 128)), 64, 1)[0:1]
    for c in range(4):
        msg[GROUP * c : GROUP * (c + 1), :] = block


def finish_kernel(sent, place, out):
    row = jnp.sum(sent[...], axis=0, keepdims=True)
    g00, g01, g11, b0, b1 = (lane_of(row, 64 + n) for n in range(5))
    shift = ridge_share * (g00 + g11) / 2 + 1e-06
    first, second = g00 + shift, g11 + shift
    determinant = first * second - g01 * g01
    c0 = -(second * b0 - g01 * b1) / determinant
    c1 = -(first * b1 - g01 * b0) / determinant
    start = pl.multiple_of(lax.axis_index("cable") * GROUP, GROUP)
    mine = sent[pl.ds(start, GROUP), :]
    turned = jnp.transpose(jnp.concatenate([mine, jnp.zeros((128 - GROUP, 128), F32)], axis=0))
    hot = (iota((128, SEG_DEV), 0).astype(F32) == place[0:1, :]).astype(F32)
    got = lax.dot_general(turned[0:64], hot, NN, precision=EXACT, preferred_element_type=F32)
    rank = place[1:2, :]
    rows = jnp.zeros((16, SEG_DEV), F32)
    for k in range(CAP):
        rows = jnp.where(rank == k, got[16 * k : 16 * k + 16], rows)
    response, before, latest = rows[0:3], rows[3:6], rows[6:9]
    out[...] = response + c0 * (response - before) + c1 * (response - latest)


def call(kernel, name, ins, outs, scratch=(), flops=0):
    vmem = pl.BlockSpec(memory_space=pltpu.VMEM)
    size = sum(a.size * 4 for a in ins) + sum(4 * o[0] * o[1] * (o[2] if len(o) > 2 else 1) for o in outs)
    got = pl.pallas_call(
        kernel,
        name=name,
        out_shape=[jax.ShapeDtypeStruct(o, F32) for o in outs],
        in_specs=[vmem] * len(ins),
        out_specs=[vmem] * len(outs),
        scratch_shapes=list(scratch),
        compiler_params=pltpu.CompilerParams(vmem_limit_bytes=16 * 1024 * 1024),
        cost_estimate=pl.CostEstimate(flops=flops, bytes_accessed=size, transcendentals=0),
    )(*ins)
    return got


def shifted(array, axis, by):
    count = lax.axis_size(axis)
    return lax.ppermute(array, axis, [(i, (i + by) % count) for i in range(count)])


def exchange(array, axes):
    return lax.all_to_all(array, axes, 0, 0, tiled=True)


def body(velocity, viscosity, disp_init, rest_shape, compliance, stencil_weights, anchor, owners):
    group = ("fx", "fz")
    flow = velocity.reshape(3, XY, SZ)
    thick = viscosity.reshape(XY, SZ)
    msg, place = call(
        pack_kernel,
        "pack",
        (disp_init, rest_shape, compliance.reshape(1, SEG_DEV), stencil_weights, anchor, owners),
        [(GROUP, 384), (8, SEG_DEV)],
        [pltpu.VMEM((32, SEG_DEV), F32)],
    )
    static = exchange(msg, group)
    sent = []
    for t in range(3):
        n = 6 if t == 2 else 3
        ny = 7 if t == 2 else 3
        outs = [(n, XY, SZ), (n, SY, SZ), (n, SY, SZ), (ny, SX, SZ), (ny, SX, SZ)]
        outs += [(XY, SLOTS), (SZ, SLOTS), (24, SLOTS)]
        if t == 2:
            outs.append((8, 128))
        field, xlo, xhi, ylo, yhi, wxy, wz, aux, *gram = call(
            functools.partial(spread_kernel, t), f"spread{t}", (static, flow, *sent), outs
        )
        beside_z = shifted(field, "fz", 1)
        yl, yu = shifted(yhi, "cable", 1), shifted(ylo, "cable", -1)
        xl, xu = shifted(xhi, "fx", 1), shifted(xlo, "fx", -1)
        ins = [thick, field, beside_z, xl, xu, yl, yu, wxy, wz, aux]
        kernel, name = functools.partial(sample_kernel, t), f"sample{t}"
        if t < 2:
            width = 3 * SLOTS + (128 if t else 0)
            (msg,) = call(kernel, name, ins, [(GROUP, width)])
            sent.append(exchange(msg, group))
        else:
            ins += [gram[0], shifted(gram[0], "cable", 2)]
            out, msg = call(
                kernel, name, ins, [(3, XY, SZ), (4 * GROUP, 128)], [pltpu.VMEM((128, 128), F32)]
            )
    last = exchange(msg, ("cable", "fx", "fz"))
    (disp_next,) = call(finish_kernel, "finish", (last, place), [(3, SEG_DEV)])
    return disp_next, out.reshape(velocity.shape)


def solution(mesh):
    segments = ("cable", "fx", "fz")
    placed = (
        P(None, "fx", "cable", "fz"),
        P("fx", "cable", "fz"),
        P(None, segments),
        P(None, segments),
        P(segments),
        P(None, None, segments),
        P(None, segments),
        P(None, segments),
    )
    return jax.shard_map(
        body,
        mesh=mesh,
        in_specs=placed,
        out_specs=(P(None, segments), P(None, "fx", "cable", "fz")),
        check_vma=False,
    )
```

time: 1480 us -> 124 us (0.08)
  waiting for transfers between devices: 437 us -> 3.88 us
  other arithmetic: 363 us -> 0 us
  local copies, waits for them, and re-layouts: 287 us -> 4.71 us
  blocking collectives: 320 us -> 81.2 us
  between operations: 24.1 us -> 0.76 us
  starting transfers between devices: 42.6 us -> 27.2 us
    unnamed x6 -> x0, waiting for transfers between devices: 412 us -> none
    scatter-add x3 -> x0, other arithmetic: 326 us -> none  [body(): forcing = jnp.zeros((3, cells), jnp.float32).at[:, cell_index.reshape(-1)...]
    gather x6 -> x0, local copies, waits for them, and re-layouts: 216 us -> none  [the longest x3 173 us: body(): picked = u_new.reshape(3, cells)[:, cell_index]]
    all_gather x3 -> x0, blocking collectives: 161 us -> none  [body(): lax.all_gather(jnp.concatenate([payload, owner_row], axis=0), ('fx', 'fz'...]
    psum x2 -> x0, blocking collectives: 159 us -> none  [body(): gram = lax.psum(partial_gram, ('cable', 'fx', 'fz'))]
    all_to_all x0 -> x4, blocking collectives: none -> 81.2 us  [exchange(): return lax.all_to_all(array, axes, 0, 0, tiled=True)]
    scatter x3 -> x0, local copies, waits for them, and re-layouts: 31.9 us -> none  [body(): compact = jnp.zeros((16, slot_total + 1), jnp.float32).at[:, slot_place]....]
    ppermute x18 -> x16, waiting for transfers between devices: 25.6 us -> 3.88 us  [shifted(): lax.ppermute(array, axis, [(i, (i + by) % count) for i in range(count)])]
  transfers between devices with their start and end apart: 21 -> 16, of which waited for: 12 -> 5; matrix products, arithmetic and copies ran while one was open for 0% -> 0% of each run, Pallas kernels for 0% -> 0%
where the time goes in v1:
time: 124 us
  blocking collectives  81.2 us (65%)
  starting transfers between devices  27.2 us (22%)
  Pallas kernels  5.78 us (5%)
  local copies, waits for them, and re-layouts  4.71 us (4%)
  waiting for transfers between devices  3.88 us (3%)
    all_to_all x4, blocking collectives, exchange(): return lax.all_to_all(array, axes, 0, 0, tiled=True)  81.2 us
    ppermute x16, starting transfers between devices, shifted(): lax.ppermute(array, axis, [(i, (i + by) % count) for i in range(count)])  27.2 us
    pallas_call x8, Pallas kernels, call(): pl.pallas_call(kernel, name=name, out_shape=[jax.ShapeDtypeStruct(o, F32)...  5.78 us
    unnamed x19, local copies, waits for them, and re-layouts  4.16 us
    ppermute x16, waiting for transfers between devices, shifted(): lax.ppermute(array, axis, [(i, (i + by) % count) for i in range(count)])  3.88 us
  transfers between devices with their start and end apart: 16, of which 5 were waited for; matrix products, arithmetic and copies ran while one was open for 0% of the time, Pallas kernels for 0%

profile of v1, /device:TPU:1, one launch (start us, length us, event | category | flops | bytes accessed | tf_op | source)
XLA Modules:
  0.0 123.6 jit_solution(451453837833755574)
XLA Ops:
  0.6 0.6 copy-done.7
  1.3 0.7 copy-done.2
  2.0 0.7 copy-done.3
  2.7 0.7 copy-done.4
  3.4 0.7 copy-done.5
  4.1 0.7 copy-done.6
  4.8 0.6 pack.1
  5.4 0.1 copy.10
  5.5 0.0 copy-start
  5.5 23.5 %all_to_all.44 = f32[64,1,384]{2,1,0:T(1,128)S(1)} all-to-all(f32[64,1,384]{2,1,0:T(1,128)S(1)} %copy.10), channel_id=1, replica_groups=mesh['cable'=4,'fx'=32,'fz'=2] {'fx','fz'}, dimensions={0} | all-to-all | bytes 196608 | tf_op jit(solution)/shard_map/all_to_all | solution.py:348
  29.0 0.0 copy-start.1
  29.0 0.5 spread0.1
  29.6 0.5 collective-permute-start
  30.1 0.2 collective-permute-start.1
  30.2 4.6 %collective-permute-start.2 = (f32[3,16,128]{2,1,0:T(8,128)S(1)}, f32[3,16,128]{2,1,0:T(8,128)S(1)}, u32[]{:S(2)}, u32[]{:S(2)}) collective-permute-start(f32[3,16,128]{2,1,0:T(8,128)S(1)} %get-tuple-element.34), channel_id=1, source_target_pairs={{0,62},{2,0},{4,2},{6,4},{8,6},{10,8},{12,10},{14,12},{16,14},{18,... | collective-permute-start | bytes 73736 | tf_op jit(solution)/shard_map/ppermute | solution.py:344
  34.9 1.3 %collective-permute-start.3 = (f32[3,8,128]{2,1,0:T(8,128)S(1)}, f32[3,8,128]{2,1,0:T(8,128)S(1)}, u32[]{:S(2)}, u32[]{:S(2)}) collective-permute-start(f32[3,8,128]{2,1,0:T(8,128)S(1)} %get-tuple-element.35), channel_id=1, source_target_pairs={{0,64},{64,128},{128,192},{192,0},{1,65},{65,129},{129,193},{193,1... | collective-permute-start | bytes 36872 | tf_op jit(solution)/shard_map/ppermute | solution.py:344
  36.2 1.4 %collective-permute-start.4 = (f32[3,8,128]{2,1,0:T(8,128)S(1)}, f32[3,8,128]{2,1,0:T(8,128)S(1)}, u32[]{:S(2)}, u32[]{:S(2)}) collective-permute-start(f32[3,8,128]{2,1,0:T(8,128)S(1)} %get-tuple-element.36), channel_id=1, source_target_pairs={{0,192},{64,0},{128,64},{192,128},{1,193},{65,1},{129,65},{193,129... | collective-permute-start | bytes 36872 | tf_op jit(solution)/shard_map/ppermute | solution.py:344
  37.6 1.1 collective-permute-done.3.refs_5_
  38.7 0.0 collective-permute-done.4.refs_6_
  38.7 0.0 collective-permute-done.1.refs_3_
  38.7 0.0 collective-permute-done.2.refs_4_
  38.7 0.5 sample0.1
  39.2 0.2 copy.11
  39.4 17.6 %all_to_all.45 = f32[64,1,768]{2,1,0:T(1,128)S(1)} all-to-all(f32[64,1,768]{2,1,0:T(1,128)S(1)} %copy.11), channel_id=1, replica_groups=mesh['cable'=4,'fx'=32,'fz'=2] {'fx','fz'}, dimensions={0} | all-to-all | bytes 393216 | tf_op jit(solution)/shard_map/all_to_all | solution.py:348
  57.0 0.7 spread1.1
  57.7 0.5 collective-permute-start.5
  58.2 0.2 collective-permute-start.6
  58.4 4.6 %collective-permute-start.7 = (f32[3,16,128]{2,1,0:T(8,128)S(1)}, f32[3,16,128]{2,1,0:T(8,128)S(1)}, u32[]{:S(2)}, u32[]{:S(2)}) collective-permute-start(f32[3,16,128]{2,1,0:T(8,128)S(1)} %get-tuple-element.42), channel_id=1, source_target_pairs={{0,62},{2,0},{4,2},{6,4},{8,6},{10,8},{12,10},{14,12},{16,14},{18,... | collective-permute-start | bytes 73736 | tf_op jit(solution)/shard_map/ppermute | solution.py:344
  63.0 1.3 %collective-permute-start.8 = (f32[3,8,128]{2,1,0:T(8,128)S(1)}, f32[3,8,128]{2,1,0:T(8,128)S(1)}, u32[]{:S(2)}, u32[]{:S(2)}) collective-permute-start(f32[3,8,128]{2,1,0:T(8,128)S(1)} %get-tuple-element.43), channel_id=1, source_target_pairs={{0,64},{64,128},{128,192},{192,0},{1,65},{65,129},{129,193},{193,1... | collective-permute-start | bytes 36872 | tf_op jit(solution)/shard_map/ppermute | solution.py:344
  64.3 1.4 %collective-permute-start.9 = (f32[3,8,128]{2,1,0:T(8,128)S(1)}, f32[3,8,128]{2,1,0:T(8,128)S(1)}, u32[]{:S(2)}, u32[]{:S(2)}) collective-permute-start(f32[3,8,128]{2,1,0:T(8,128)S(1)} %get-tuple-element.44), channel_id=1, source_target_pairs={{0,192},{64,0},{128,64},{192,128},{1,193},{65,1},{129,65},{193,129... | collective-permute-start | bytes 36872 | tf_op jit(solution)/shard_map/ppermute | solution.py:344
  65.8 1.1 collective-permute-done.8.refs_5_
  66.8 0.0 collective-permute-done.9.refs_6_
  66.9 0.5 sample1.1
  67.4 0.2 copy.12
  67.7 18.3 %all_to_all.46 = f32[64,1,896]{2,1,0:T(1,128)S(1)} all-to-all(f32[64,1,896]{2,1,0:T(1,128)S(1)} %copy.12), channel_id=1, replica_groups=mesh['cable'=4,'fx'=32,'fz'=2] {'fx','fz'}, dimensions={0} | all-to-all | bytes 458752 | tf_op jit(solution)/shard_map/all_to_all | solution.py:348
  86.0 1.0 spread2.1
  87.0 0.4 collective-permute-start.10
  87.4 0.4 collective-permute-start.11
  87.8 4.4 %collective-permute-start.12 = (f32[6,16,128]{2,1,0:T(8,128)S(1)}, f32[6,16,128]{2,1,0:T(8,128)S(1)}, u32[]{:S(2)}, u32[]{:S(2)}) collective-permute-start(f32[6,16,128]{2,1,0:T(8,128)S(1)} %get-tuple-element.50), channel_id=1, source_target_pairs={{0,62},{2,0},{4,2},{6,4},{8,6},{10,8},{12,10},{14,12},{16,14},{18,... | collective-permute-start | bytes 147464 | tf_op jit(solution)/shard_map/ppermute | solution.py:344
  92.1 2.9 %collective-permute-start.15 = (f32[8,128]{1,0:T(8,128)S(1)}, f32[8,128]{1,0:T(8,128)S(1)}, u32[]{:S(2)}, u32[]{:S(2)}) collective-permute-start(f32[8,128]{1,0:T(8,128)S(1)} %get-tuple-element.56.refs_10_), channel_id=1, source_target_pairs={{0,128},{64,192},{128,0},{192,64},{1,129},{65,193},{129,1},{193,65... | collective-permute-start | bytes 12296 | tf_op jit(solution)/shard_map/ppermute | solution.py:344
  95.1 0.4 collective-permute-start.13
  95.5 0.6 collective-permute-done.15.refs_11_
  96.1 2.7 %collective-permute-start.14 = (f32[7,8,128]{2,1,0:T(8,128)S(1)}, f32[7,8,128]{2,1,0:T(8,128)S(1)}, u32[]{:S(2)}, u32[]{:S(2)}) collective-permute-start(f32[7,8,128]{2,1,0:T(8,128)S(1)} %get-tuple-element.52), channel_id=1, source_target_pairs={{0,192},{64,0},{128,64},{192,128},{1,193},{65,1},{129,65},{193,129... | collective-permute-start | bytes 86024 | tf_op jit(solution)/shard_map/ppermute | solution.py:344
  98.8 0.1 collective-permute-done.13.refs_5_
  99.0 0.8 collective-permute-done.14.refs_6_
  99.8 1.1 sample2.1
  100.9 21.9 %all_to_all.47 = f32[256,1,128]{2,1,0:T(1,128)S(1)} all-to-all(f32[256,1,128]{2,1,0:T(1,128)S(1)} %bitcast.35), channel_id=1, replica_groups=mesh['cable'=4,'fx'=32,'fz'=2] {'cable','fx','fz'}, dimensions={0} | all-to-all | bytes 262144 | tf_op jit(solution)/shard_map/all_to_all | solution.py:348
  122.8 0.8 finish.1
  (18 shorter events, 0.1 us)
Async XLA Ops:
  0.6 0.7 copy-start.7
  1.3 0.7 copy-start.2
  2.0 0.7 copy-start.3
  2.7 0.7 copy-start.4
  3.4 0.7 copy-start.5
  4.1 0.7 copy-start.6
  5.5 23.5 %copy-start = (f32[3,8,16,128]{3,2,1,0:T(8,128)S(1)}, f32[3,8,16,128]{3,2,1,0:T(8,128)}, u32[]{:S(2)}) copy-start(f32[3,8,16,128]{3,2,1,0:T(8,128)} %param.8) | copy-start | bytes 589828
  29.0 9.7 %copy-start.1 = (f32[8,16,128]{2,1,0:T(8,128)S(1)}, f32[8,16,128]{2,1,0:T(8,128)}, u32[]{:S(2)}) copy-start(f32[8,16,128]{2,1,0:T(8,128)} %param.9) | copy-start | bytes 196612
  29.6 9.1 %collective-permute-start = (f32[3,128,128]{2,1,0:T(8,128)S(1)}, f32[3,128,128]{2,1,0:T(8,128)S(1)}, u32[]{:S(2)}, u32[]{:S(2)}) collective-permute-start(f32[3,128,128]{2,1,0:T(8,128)S(1)} %get-tuple-element.32.refs_1_), channel_id=1, source_target_pairs={{0,1},{1,0},{2,3},{3,2},{4,5},{5,4},{6,7},{7,6},{8,9},{9,8},{10,11... | collective-permute-start | bytes 589832 | tf_op jit(solution)/shard_map/ppermute | solution.py:344
  30.1 8.6 %collective-permute-start.1 = (f32[3,16,128]{2,1,0:T(8,128)S(1)}, f32[3,16,128]{2,1,0:T(8,128)S(1)}, u32[]{:S(2)}, u32[]{:S(2)}) collective-permute-start(f32[3,16,128]{2,1,0:T(8,128)S(1)} %get-tuple-element.33), channel_id=1, source_target_pairs={{0,2},{2,4},{4,6},{6,8},{8,10},{10,12},{12,14},{14,16},{16,18},{18... | collective-permute-start | bytes 73736 | tf_op jit(solution)/shard_map/ppermute | solution.py:344
  30.2 8.5 %collective-permute-start.2 = (f32[3,16,128]{2,1,0:T(8,128)S(1)}, f32[3,16,128]{2,1,0:T(8,128)S(1)}, u32[]{:S(2)}, u32[]{:S(2)}) collective-permute-start(f32[3,16,128]{2,1,0:T(8,128)S(1)} %get-tuple-element.34), channel_id=1, source_target_pairs={{0,62},{2,0},{4,2},{6,4},{8,6},{10,8},{12,10},{14,12},{16,14},{18,... | collective-permute-start | bytes 73736 | tf_op jit(solution)/shard_map/ppermute | solution.py:344
  34.9 3.8 %collective-permute-start.3 = (f32[3,8,128]{2,1,0:T(8,128)S(1)}, f32[3,8,128]{2,1,0:T(8,128)S(1)}, u32[]{:S(2)}, u32[]{:S(2)}) collective-permute-start(f32[3,8,128]{2,1,0:T(8,128)S(1)} %get-tuple-element.35), channel_id=1, source_target_pairs={{0,64},{64,128},{128,192},{192,0},{1,65},{65,129},{129,193},{193,1... | collective-permute-start | bytes 36872 | tf_op jit(solution)/shard_map/ppermute | solution.py:344
  36.2 2.5 %collective-permute-start.4 = (f32[3,8,128]{2,1,0:T(8,128)S(1)}, f32[3,8,128]{2,1,0:T(8,128)S(1)}, u32[]{:S(2)}, u32[]{:S(2)}) collective-permute-start(f32[3,8,128]{2,1,0:T(8,128)S(1)} %get-tuple-element.36), channel_id=1, source_target_pairs={{0,192},{64,0},{128,64},{192,128},{1,193},{65,1},{129,65},{193,129... | collective-permute-start | bytes 36872 | tf_op jit(solution)/shard_map/ppermute | solution.py:344
  57.7 9.1 %collective-permute-start.5 = (f32[3,128,128]{2,1,0:T(8,128)S(1)}, f32[3,128,128]{2,1,0:T(8,128)S(1)}, u32[]{:S(2)}, u32[]{:S(2)}) collective-permute-start(f32[3,128,128]{2,1,0:T(8,128)S(1)} %get-tuple-element.40.refs_1_), channel_id=1, source_target_pairs={{0,1},{1,0},{2,3},{3,2},{4,5},{5,4},{6,7},{7,6},{8,9},{9,8},{10,11... | collective-permute-start | bytes 589832 | tf_op jit(solution)/shard_map/ppermute | solution.py:344
  58.2 8.6 %collective-permute-start.6 = (f32[3,16,128]{2,1,0:T(8,128)S(1)}, f32[3,16,128]{2,1,0:T(8,128)S(1)}, u32[]{:S(2)}, u32[]{:S(2)}) collective-permute-start(f32[3,16,128]{2,1,0:T(8,128)S(1)} %get-tuple-element.41), channel_id=1, source_target_pairs={{0,2},{2,4},{4,6},{6,8},{8,10},{10,12},{12,14},{14,16},{16,18},{18... | collective-permute-start | bytes 73736 | tf_op jit(solution)/shard_map/ppermute | solution.py:344
  58.4 8.5 %collective-permute-start.7 = (f32[3,16,128]{2,1,0:T(8,128)S(1)}, f32[3,16,128]{2,1,0:T(8,128)S(1)}, u32[]{:S(2)}, u32[]{:S(2)}) collective-permute-start(f32[3,16,128]{2,1,0:T(8,128)S(1)} %get-tuple-element.42), channel_id=1, source_target_pairs={{0,62},{2,0},{4,2},{6,4},{8,6},{10,8},{12,10},{14,12},{16,14},{18,... | collective-permute-start | bytes 73736 | tf_op jit(solution)/shard_map/ppermute | solution.py:344
  63.0 3.8 %collective-permute-start.8 = (f32[3,8,128]{2,1,0:T(8,128)S(1)}, f32[3,8,128]{2,1,0:T(8,128)S(1)}, u32[]{:S(2)}, u32[]{:S(2)}) collective-permute-start(f32[3,8,128]{2,1,0:T(8,128)S(1)} %get-tuple-element.43), channel_id=1, source_target_pairs={{0,64},{64,128},{128,192},{192,0},{1,65},{65,129},{129,193},{193,1... | collective-permute-start | bytes 36872 | tf_op jit(solution)/shard_map/ppermute | solution.py:344
  64.3 2.5 %collective-permute-start.9 = (f32[3,8,128]{2,1,0:T(8,128)S(1)}, f32[3,8,128]{2,1,0:T(8,128)S(1)}, u32[]{:S(2)}, u32[]{:S(2)}) collective-permute-start(f32[3,8,128]{2,1,0:T(8,128)S(1)} %get-tuple-element.44), channel_id=1, source_target_pairs={{0,192},{64,0},{128,64},{192,128},{1,193},{65,1},{129,65},{193,129... | collective-permute-start | bytes 36872 | tf_op jit(solution)/shard_map/ppermute | solution.py:344
  87.0 12.9 %collective-permute-start.10 = (f32[6,128,128]{2,1,0:T(8,128)S(1)}, f32[6,128,128]{2,1,0:T(8,128)S(1)}, u32[]{:S(2)}, u32[]{:S(2)}) collective-permute-start(f32[6,128,128]{2,1,0:T(8,128)S(1)} %get-tuple-element.48.refs_1_), channel_id=1, source_target_pairs={{0,1},{1,0},{2,3},{3,2},{4,5},{5,4},{6,7},{7,6},{8,9},{9,8},{10,11... | collective-permute-start | bytes 1179656 | tf_op jit(solution)/shard_map/ppermute | solution.py:344
  87.4 12.5 %collective-permute-start.11 = (f32[6,16,128]{2,1,0:T(8,128)S(1)}, f32[6,16,128]{2,1,0:T(8,128)S(1)}, u32[]{:S(2)}, u32[]{:S(2)}) collective-permute-start(f32[6,16,128]{2,1,0:T(8,128)S(1)} %get-tuple-element.49), channel_id=1, source_target_pairs={{0,2},{2,4},{4,6},{6,8},{8,10},{10,12},{12,14},{14,16},{16,18},{18... | collective-permute-start | bytes 147464 | tf_op jit(solution)/shard_map/ppermute | solution.py:344
  87.8 12.1 %collective-permute-start.12 = (f32[6,16,128]{2,1,0:T(8,128)S(1)}, f32[6,16,128]{2,1,0:T(8,128)S(1)}, u32[]{:S(2)}, u32[]{:S(2)}) collective-permute-start(f32[6,16,128]{2,1,0:T(8,128)S(1)} %get-tuple-element.50), channel_id=1, source_target_pairs={{0,62},{2,0},{4,2},{6,4},{8,6},{10,8},{12,10},{14,12},{16,14},{18,... | collective-permute-start | bytes 147464 | tf_op jit(solution)/shard_map/ppermute | solution.py:344
  92.1 4.0 %collective-permute-start.15 = (f32[8,128]{1,0:T(8,128)S(1)}, f32[8,128]{1,0:T(8,128)S(1)}, u32[]{:S(2)}, u32[]{:S(2)}) collective-permute-start(f32[8,128]{1,0:T(8,128)S(1)} %get-tuple-element.56.refs_10_), channel_id=1, source_target_pairs={{0,128},{64,192},{128,0},{192,64},{1,129},{65,193},{129,1},{193,65... | collective-permute-start | bytes 12296 | tf_op jit(solution)/shard_map/ppermute | solution.py:344
  95.1 3.9 %collective-permute-start.13 = (f32[7,8,128]{2,1,0:T(8,128)S(1)}, f32[7,8,128]{2,1,0:T(8,128)S(1)}, u32[]{:S(2)}, u32[]{:S(2)}) collective-permute-start(f32[7,8,128]{2,1,0:T(8,128)S(1)} %get-tuple-element.51), channel_id=1, source_target_pairs={{0,64},{64,128},{128,192},{192,0},{1,65},{65,129},{129,193},{193,1... | collective-permute-start | bytes 86024 | tf_op jit(solution)/shard_map/ppermute | solution.py:344
  96.1 3.7 %collective-permute-start.14 = (f32[7,8,128]{2,1,0:T(8,128)S(1)}, f32[7,8,128]{2,1,0:T(8,128)S(1)}, u32[]{:S(2)}, u32[]{:S(2)}) collective-permute-start(f32[7,8,128]{2,1,0:T(8,128)S(1)} %get-tuple-element.52), channel_id=1, source_target_pairs={{0,192},{64,0},{128,64},{192,128},{1,193},{65,1},{129,65},{193,129... | collective-permute-start | bytes 86024 | tf_op jit(solution)/shard_map/ppermute | solution.py:344

commit v2 on v1

--- a/solution.py
+++ b/solution.py
@@ -1,4 +1,5 @@
 import functools
+import math
 
 import jax
 import jax.numpy as jnp
@@ -25,7 +26,11 @@
 SX, SY, SZ = 8, 16, 128
 XY = SX * SY
 
-R_W, R_A, R_D0, R_REST, R_CR, R_CODE = 0, 12, 15, 18, 21, 22
+R_W, R_CELL, R_D0, R_REST, R_CR, R_CODE = 0, 12, 13, 16, 19, 20
+HEIGHT = (16, 24, 24)
+SETS = 3
+BASE = (0, 192, 480)
+FIELDS = 768
 
 
 def split(x):
@@ -42,66 +47,86 @@
     return lax.broadcasted_iota(jnp.int32, shape, dim)
 
 
-def pack_kernel(disp, rest, comp, weights, anchor, owner, msg, place, fields):
+def pack_kernel(*refs):
+    far, (msg, place, xlo, xhi), near, fields, turn, sems = refs[0:7], refs[7:11], refs[11:17], refs[17], refs[18], refs[19]
+    copies = [pltpu.make_async_copy(far[n], near[n], sems.at[n]) for n in (5, 4, 3, 0, 1, 2)]
+    copies.append(pltpu.make_async_copy(far[6].at[:, 0:SY, :], xlo, sems.at[6]))
+    copies.append(pltpu.make_async_copy(far[6].at[:, XY - SY : XY, :], xhi, sems.at[7]))
+    for copy in copies:
+        copy.start()
+    disp, rest, comp, weights, anchor, owner = near
     fz_n, fx_n, cable_n = lax.axis_size("fz"), lax.axis_size("fx"), lax.axis_size("cable")
     device = (lax.axis_index("cable") * fx_n + lax.axis_index("fx")) * fz_n + lax.axis_index("fz")
     position = (device * SEG_DEV + iota((1, SEG_DEV), 1)).astype(F32)
     ramp = 1.0 + 2.0 * position / (SEG_DEV * fz_n * fx_n * cable_n)
     dest = iota((GROUP, SEG_DEV), 0)
     earlier = (iota((SEG_DEV, SEG_DEV), 0) < iota((SEG_DEV, SEG_DEV), 1)).astype(F32)
-    hots, ranks, codes = [], [], []
+    fields[...] = jnp.zeros_like(fields)
+    turn[...] = jnp.zeros_like(turn)
+    place[...] = jnp.zeros_like(place)
+    for copy in copies:
+        copy.wait()
+    ranks, codes = [], []
     for t in range(3):
         own = owner[t : t + 1, :]
         hot = (dest == own).astype(F32)
         before = lax.dot_general(hot, earlier, NN, preferred_element_type=F32)
         rank = jnp.sum(hot * before, axis=0, keepdims=True)
-        hots.append(hot)
         ranks.append(rank)
         codes.append(own.astype(F32) * CAP + rank)
-    fields[...] = jnp.zeros_like(fields)
     fields[R_D0 : R_D0 + 3, :] = disp[...]
     fields[R_REST : R_REST + 3, :] = rest[...]
     fields[R_CR : R_CR + 1, :] = comp[...] * ramp
-    fields[R_CODE : R_CODE + 1, :] = codes[0]
-    fields[R_CODE + 1 : R_CODE + 2, :] = codes[1]
+    fields[R_CODE : R_CODE + 1, :] = codes[0] + SLOTS * codes[1]
     for t in range(3):
-        cell = anchor[t : t + 1, :]
+        own = owner[t : t + 1, :]
         fields[R_W : R_W + 12, :] = weights[t]
-        fields[R_A : R_A + 1, :] = (cell >> 11).astype(F32)
-        fields[R_A + 1 : R_A + 2, :] = ((cell >> 7) & (SY - 1)).astype(F32)
-        fields[R_A + 2 : R_A + 3, :] = (cell & (SZ - 1)).astype(F32)
-        now = fields[...]
+        fields[R_CELL : R_CELL + 1, :] = anchor[t : t + 1, :].astype(F32)
+        now = fields[0 : HEIGHT[t], :]
         placed = jnp.concatenate([jnp.where(ranks[t] == k, now, 0.0) for k in range(CAP)], axis=0)
-        msg[:, 128 * t : 128 * t + 128] = lax.dot_general(
-            hots[t], placed, NT, precision=EXACT, preferred_element_type=F32
-        )
-    place[...] = jnp.zeros_like(place)
+        for j, step in enumerate((0, fz_n, -fz_n)):
+            start = BASE[t] + CAP * HEIGHT[t] * j
+            turn[start : start + CAP * HEIGHT[t], 0:GROUP] = lax.dot_general(
+                placed, (dest == own + step).astype(F32), NT, precision=EXACT, preferred_element_type=F32
+            )
+    for n in range(FIELDS // 128):
+        msg[:, 128 * n : 128 * n + 128] = jnp.transpose(turn[128 * n : 128 * n + 128, :])[0:GROUP]
     place[0:1, :] = owner[2:3, :].astype(F32)
     place[1:2, :] = ranks[2]
 
 
-def slot_rows(block):
-    wide = jnp.concatenate([block, jnp.zeros((128 - GROUP, 128), F32)], axis=0)
-    turned = jnp.transpose(wide)
-    low = turned[0:32] + pltpu.roll(turned[32:64], 64, 1)
-    high = turned[64:96] + pltpu.roll(turned[96:128], 64, 1)
-    return jnp.concatenate([low, high], axis=1)
-
-
-def along(rows, first, start, extent):
-    at = iota((extent, SLOTS), 0).astype(F32) - rows[start : start + 1]
-    total = jnp.zeros((extent, SLOTS), F32)
+def turn_static(static, turned, t):
+    first = BASE[t] // 128
+    last = (BASE[t] + SETS * CAP * HEIGHT[t] + 127) // 128
+    for n in range(first, last):
+        block = static[:, 128 * n : 128 * n + 128]
+        wide = jnp.concatenate([block, jnp.zeros((128 - GROUP, 128), F32)], axis=0)
+        turned[128 * n : 128 * n + 128, :] = jnp.transpose(wide)
+
+
+def slot_rows(turned, t, j):
+    height = HEIGHT[t]
+    start = BASE[t] + CAP * height * j
+    part = [turned[start + height * k : start + height * (k + 1), :] for k in range(CAP)]
+    halves = [part[2 * n] + pltpu.roll(part[2 * n + 1], 64, 1) for n in range(2)]
+    return jnp.concatenate(halves, axis=1)
+
+
+def along(rows, first, at):
+    total = jnp.zeros(at.shape, F32)
     for i in range(4):
         total = jnp.where(at == i, rows[first + i : first + i + 1], total)
     return total
 
 
-def tables(rows):
-    wx = along(rows, R_W, R_A, SX)
-    wy = along(rows, R_W + 4, R_A + 1, SY)
-    wz = along(rows, R_W + 8, R_A + 2, SZ)
-    wxy = jnp.concatenate([wx[x : x + 1] * wy for x in range(SX)], axis=0)
-    return wxy, wz
+def tables(rows, plane=None):
+    cell = rows[R_CELL : R_CELL + 1].astype(jnp.int32)
+    wy = along(rows, R_W + 4, iota((SY, SLOTS), 0) - ((cell >> 7) & (SY - 1)))
+    wz = along(rows, R_W + 8, iota((SZ, SLOTS), 0) - (cell & (SZ - 1)))
+    if plane is not None:
+        return along(rows, R_W, plane - (cell >> 11)) * wy, wz
+    wx = along(rows, R_W, iota((SX, SLOTS), 0) - (cell >> 11))
+    return jnp.concatenate([wx[x : x + 1] * wy for x in range(SX)], axis=0), wz
 
 
 def spread(wxy2, wz, disp):
@@ -110,7 +135,7 @@
 
 def look_up(sent, code):
     low_half = iota((1, 128), 1) < 64
-    label = (iota((GROUP, SLOTS), 0) * CAP + iota((GROUP, SLOTS), 1) // 64).astype(F32)
+    label = iota((GROUP, SLOTS), 0) * CAP + iota((GROUP, SLOTS), 1) // 64
     halves = [[None] * 2 for _ in range(3)]
     for half in range(2):
         piece = code[:, 128 * half : 128 * half + 128]
@@ -136,54 +161,68 @@
     return [rows[R_REST + c : R_REST + c + 1] + cr * sampled[c] for c in range(3)]
 
 
-def put_faces(field, first, xlo, xhi, ylo, yhi):
-    for c in range(3):
-        xlo[first + c] = field[first + c, 0:SY, :]
-        xhi[first + c] = field[first + c, XY - SY : XY, :]
-        ylo[first + c] = field[first + c, pl.ds(0, SX, stride=SY), :]
-        yhi[first + c] = field[first + c, pl.ds(SY - 1, SX, stride=SY), :]
+def displacements(t, rows, sent):
+    first = [rows[R_D0 + c : R_D0 + c + 1] for c in range(3)]
+    if t == 0:
+        return [first], []
+    code = rows[R_CODE : R_CODE + 1].astype(jnp.int32)
+    before = responses(rows, look_up(sent[0], code & (SLOTS - 1)))
+    gap = [before[c] - first[c] for c in range(3)]
+    second = [first[c] + relaxation * gap[c] for c in range(3)]
+    if t == 1:
+        return [second], [second, gap]
+    latest = responses(rows, look_up(sent[1], code >> 8))
+    change = [latest[c] - before[c] for c in range(3)]
+    return [latest, change], [latest, change, gap, [latest[c] - second[c] for c in range(3)], before]
 
 
 def spread_kernel(t, *refs):
-    static, velocity = refs[0:2]
-    sent = refs[2 : 2 + t]
-    field, xlo, xhi, ylo, yhi, wxy_out, wz_out, aux = refs[2 + t : 10 + t]
-    rows = slot_rows(static[:, 128 * t : 128 * t + 128])
+    static, velocity, far_l, far_u = refs[0:4]
+    sent = refs[4 : 4 + t]
+    field, xl, xu, wxy_out, wz_out, aux = refs[4 + t : 10 + t]
+    faces, turned = refs[10 + t : -1], refs[-1]
+    turn_static(static, turned, t)
+    rows = slot_rows(turned, t, 0)
     wxy, wz = tables(rows)
     wxy_out[...] = wxy
     wz_out[...] = wz
     wxy2 = split(wxy)
-    first = [rows[R_D0 + c : R_D0 + c + 1] for c in range(3)]
-    aux[...] = jnp.zeros_like(aux)
-    if t == 0:
-        bases = [first]
-    else:
-        before = responses(rows, look_up(sent[0], rows[R_CODE : R_CODE + 1]))
-        gap = [before[c] - first[c] for c in range(3)]
-        second = [first[c] + relaxation * gap[c] for c in range(3)]
-        bases = [second]
-        kept = [second, gap]
-        if t == 2:
-            latest = responses(rows, look_up(sent[1], rows[R_CODE + 1 : R_CODE + 2]))
-            change = [latest[c] - before[c] for c in range(3)]
-            bases = [latest, change]
-            kept = [latest, change, gap, [latest[c] - second[c] for c in range(3)], before]
+    bases, kept = displacements(t, rows, sent)
+    for n, base in enumerate(bases):
+        for c in range(3):
+            forced = spread(wxy2, wz, base[c])
+            field[3 * n + c] = velocity[c] + forced if n == 0 else forced
+    if t > 0:
+        aux[...] = jnp.zeros_like(aux)
         for n, group in enumerate(kept):
             for c in range(3):
                 aux[3 * n + c : 3 * n + c + 1, :] = group[c]
         aux[16:20, :] = rows[R_REST : R_REST + 4]
-    for n, base in enumerate(bases):
-        for c in range(3):
-            forced = spread(wxy2, wz, base[c])
-            field[3 * n + c] = velocity[c] + forced if n == 0 else forced
-        put_faces(field, 3 * n, xlo, xhi, ylo, yhi)
-    if t == 2:
-        gram = refs[10 + t]
-        total = jnp.sum(sent[1][:, 3 * SLOTS : 3 * SLOTS + 128], axis=0, keepdims=True)
-        total = jnp.broadcast_to(total, (8, 128))
-        gram[...] = total
-        ylo[6] = total
-        yhi[6] = total
+    fx = lax.axis_index("fx")
+    beside = ((xl, far_l, SX - 1, fx > 0), (xu, far_u, 0, fx < lax.axis_size("fx") - 1))
+    for j, (out, far, plane, inside) in enumerate(beside):
+        rows = slot_rows(turned, t, 1 + j)
+        wxy, wz = tables(rows, plane)
+        wxy2 = split(wxy)
+        bases, _ = displacements(t, rows, sent)
+        for n, base in enumerate(bases):
+            for c in range(3):
+                forced = spread(wxy2, wz, base[c])
+                out[3 * n + c] = jnp.where(inside, far[c], 0.0) + forced if n == 0 else forced
+    low = [field[n, pl.ds(0, SX, stride=SY), :] for n in range(3 * len(bases))]
+    high = [field[n, pl.ds(SY - 1, SX, stride=SY), :] for n in range(3 * len(bases))]
+    if t < 2:
+        for c in range(3):
+            faces[0][c] = low[c]
+            faces[1][c] = high[c]
+        return
+    total = jnp.sum(sent[1][:, 3 * SLOTS : 3 * SLOTS + 128], axis=0, keepdims=True)
+    total = jnp.broadcast_to(total, (8, 128))
+    me = lax.axis_index("cable")
+    for e in range(4):
+        for n in range(6):
+            faces[0][e, n] = jnp.where(me < e, high[n], low[n])
+        faces[0][e, 6] = total
 
 
 def wake(u, beside_z, xl, xu, yl, yu, viscosity):
@@ -233,35 +272,39 @@
 
 
 def sample_kernel(t, *refs):
-    viscosity, field, beside_z, xl, xu, yl, yu, wxy, wz, aux = refs[0:10]
-    inside = (
-        lax.axis_index("fx") > 0,
-        lax.axis_index("fx") < lax.axis_size("fx") - 1,
-        lax.axis_index("cable") > 0,
-        lax.axis_index("cable") < lax.axis_size("cable") - 1,
-    )
+    viscosity, field, beside_z, xl, xu, wxy, wz, aux = refs[0:8]
+    me = lax.axis_index("cable")
+    last = lax.axis_size("cable") - 1
 
     def whole(ref):
         if t < 2:
             return [ref[c] for c in range(3)]
         return [ref[c] + coef * ref[3 + c] for c in range(3)]
 
-    if t == 2:
-        own, across = refs[10:12]
-        gram = own[0:1] + yl[6][0:1] + yu[6][0:1] + across[0:1]
-        square, target = lane_of(gram, 0), lane_of(gram, 1)
+    if t < 2:
+        yl = [jnp.where(me > 0, refs[8][c], 0.0) for c in range(3)]
+        yu = [jnp.where(me < last, refs[9][c], 0.0) for c in range(3)]
+    else:
+        got = refs[8]
+        gram = got[0, 6] + got[1, 6] + got[2, 6] + got[3, 6]
+        square, target = lane_of(gram[0:1], 0), lane_of(gram[0:1], 1)
         coef = -target / (square + (ridge_share * square + 1e-06))
+        yl, yu = [], []
+        for c in range(3):
+            below, above = jnp.zeros((SX, SZ), F32), jnp.zeros((SX, SZ), F32)
+            for e in range(4):
+                face = got[e, c] + coef * got[e, 3 + c]
+                below = jnp.where(me == e + 1, face, below)
+                above = jnp.where(me == e - 1, face, above)
+            yl.append(below)
+            yu.append(above)
     u = whole(field)
-    faces = [
-        [jnp.where(ok, face, 0.0) for face in whole(ref)]
-        for ok, ref in zip(inside, (xl, xu, yl, yu))
-    ]
+    faces = [whole(xl), whole(xu), yl, yu]
     new = wake(u, whole(beside_z), *faces, viscosity[...])
     sampled = sample(new, wxy[...], wz[...])
     if t == 0:
-        msg = refs[10]
-        for c in range(3):
-            msg[:, SLOTS * c : SLOTS * (c + 1)] = jnp.broadcast_to(sampled[c], (GROUP, SLOTS))
+        for c in range(3):
+            refs[10][:, SLOTS * c : SLOTS * (c + 1)] = jnp.broadcast_to(sampled[c], (GROUP, SLOTS))
         return
 
     def kept(n):
@@ -279,7 +322,7 @@
         row = in_lanes([total_of(v0, v0), total_of(v0, gap)])
         msg[:, 3 * SLOTS : 3 * SLOTS + 128] = jnp.broadcast_to(row, (GROUP, 128))
         return
-    out, msg, turn = refs[12:15]
+    out, msg, turn = refs[9:12]
     for c in range(3):
         out[c] = new[c]
     latest, change, gap0, gap1, before = (kept(n) for n in range(5))
@@ -323,20 +366,18 @@
     out[...] = response + c0 * (response - before) + c1 * (response - latest)
 
 
-def call(kernel, name, ins, outs, scratch=(), flops=0):
-    vmem = pl.BlockSpec(memory_space=pltpu.VMEM)
-    size = sum(a.size * 4 for a in ins) + sum(4 * o[0] * o[1] * (o[2] if len(o) > 2 else 1) for o in outs)
-    got = pl.pallas_call(
+def call(kernel, name, ins, outs, scratch=(), space=pltpu.VMEM):
+    size = sum(a.size * 4 for a in ins) + sum(4 * math.prod(o) for o in outs)
+    return pl.pallas_call(
         kernel,
         name=name,
         out_shape=[jax.ShapeDtypeStruct(o, F32) for o in outs],
-        in_specs=[vmem] * len(ins),
-        out_specs=[vmem] * len(outs),
+        in_specs=[pl.BlockSpec(memory_space=space)] * len(ins),
+        out_specs=[pl.BlockSpec(memory_space=pltpu.VMEM)] * len(outs),
         scratch_shapes=list(scratch),
         compiler_params=pltpu.CompilerParams(vmem_limit_bytes=16 * 1024 * 1024),
-        cost_estimate=pl.CostEstimate(flops=flops, bytes_accessed=size, transcendentals=0),
+        cost_estimate=pl.CostEstimate(flops=0, bytes_accessed=size, transcendentals=0),
     )(*ins)
-    return got
 
 
 def shifted(array, axis, by):
@@ -352,36 +393,38 @@
     group = ("fx", "fz")
     flow = velocity.reshape(3, XY, SZ)
     thick = viscosity.reshape(XY, SZ)
-    msg, place = call(
+    ins = (disp_init, rest_shape, compliance.reshape(1, SEG_DEV), stencil_weights, anchor, owners)
+    msg, place, xlo, xhi = call(
         pack_kernel,
         "pack",
-        (disp_init, rest_shape, compliance.reshape(1, SEG_DEV), stencil_weights, anchor, owners),
-        [(GROUP, 384), (8, SEG_DEV)],
-        [pltpu.VMEM((32, SEG_DEV), F32)],
+        (*ins, flow),
+        [(GROUP, FIELDS), (8, SEG_DEV), (3, SY, SZ), (3, SY, SZ)],
+        [pltpu.VMEM(a.shape, a.dtype) for a in ins]
+        + [pltpu.VMEM((24, SEG_DEV), F32), pltpu.VMEM((FIELDS, 128), F32), pltpu.SemaphoreType.DMA((8,))],
+        pltpu.HBM,
     )
     static = exchange(msg, group)
+    far_l, far_u = shifted(xhi, "fx", 1), shifted(xlo, "fx", -1)
     sent = []
     for t in range(3):
         n = 6 if t == 2 else 3
-        ny = 7 if t == 2 else 3
-        outs = [(n, XY, SZ), (n, SY, SZ), (n, SY, SZ), (ny, SX, SZ), (ny, SX, SZ)]
-        outs += [(XY, SLOTS), (SZ, SLOTS), (24, SLOTS)]
-        if t == 2:
-            outs.append((8, 128))
-        field, xlo, xhi, ylo, yhi, wxy, wz, aux, *gram = call(
-            functools.partial(spread_kernel, t), f"spread{t}", (static, flow, *sent), outs
+        outs = [(n, XY, SZ), (n, SY, SZ), (n, SY, SZ), (XY, SLOTS), (SZ, SLOTS), (24, SLOTS)]
+        outs += [(4, 7, SX, SZ)] if t == 2 else [(3, SX, SZ)] * 2
+        field, xl, xu, wxy, wz, aux, *faces = call(
+            functools.partial(spread_kernel, t),
+            f"spread{t}",
+            (static, flow, far_l, far_u, *sent),
+            outs,
+            [pltpu.VMEM((FIELDS, 128), F32)],
         )
-        beside_z = shifted(field, "fz", 1)
-        yl, yu = shifted(yhi, "cable", 1), shifted(ylo, "cable", -1)
-        xl, xu = shifted(xhi, "fx", 1), shifted(xlo, "fx", -1)
-        ins = [thick, field, beside_z, xl, xu, yl, yu, wxy, wz, aux]
+        ins = [thick, field, shifted(field, "fz", 1), xl, xu, wxy, wz, aux]
         kernel, name = functools.partial(sample_kernel, t), f"sample{t}"
         if t < 2:
-            width = 3 * SLOTS + (128 if t else 0)
-            (msg,) = call(kernel, name, ins, [(GROUP, width)])
+            ins += [shifted(faces[1], "cable", 1), shifted(faces[0], "cable", -1)]
+            (msg,) = call(kernel, name, ins, [(GROUP, 3 * SLOTS + (128 if t else 0))])
             sent.append(exchange(msg, group))
         else:
-            ins += [gram[0], shifted(gram[0], "cable", 2)]
+            ins.append(exchange(faces[0], "cable"))
             out, msg = call(
                 kernel, name, ins, [(3, XY, SZ), (4 * GROUP, 128)], [pltpu.VMEM((128, 128), F32)]
             )

time: 124 us -> 113 us (0.911)
  blocking collectives: 81.2 us -> 63.6 us
  waiting for transfers between devices: 3.88 us -> 9.71 us
  starting transfers between devices: 27.2 us -> 24.8 us
  Pallas kernels: 5.78 us -> 7.73 us
    all_to_all x4, blocking collectives: 81.2 us -> 63.6 us  [exchange(): return lax.all_to_all(array, axes, 0, 0, tiled=True)]
    ppermute x16 -> x9, starting transfers between devices: 27.2 us -> 11.8 us  [shifted(): lax.ppermute(array, axis, [(i, (i + by) % count) for i in range(count)])]
    all_to_all x0 -> x1, starting transfers between devices: none -> 13 us  [exchange(): return lax.all_to_all(array, axes, 0, 0, tiled=True)]
    all_to_all x0 -> x1, waiting for transfers between devices: none -> 6.84 us  [exchange(): return lax.all_to_all(array, axes, 0, 0, tiled=True)]
    pallas_call x8, Pallas kernels: 5.78 us -> 7.73 us  [call(): pl.pallas_call(kernel, name=name, out_shape=[jax.ShapeDtypeStruct(o, F32)...]
    ppermute x16 -> x9, waiting for transfers between devices: 3.88 us -> 2.87 us  [shifted(): lax.ppermute(array, axis, [(i, (i + by) % count) for i in range(count)])]
    unnamed x19 -> x21, local copies, waits for them, and re-layouts: 4.16 us -> 4.43 us
  transfers between devices with their start and end apart: 16 -> 10, of which waited for: 5 -> 5; matrix products, arithmetic and copies ran while one was open for 0% -> 0% of each run, Pallas kernels for 0% -> 0%
where the time goes in v2:
time: 113 us; the launch traced here: 112 us
  blocking collectives  63.6 us (56%)
  starting transfers between devices  24.8 us (22%)
  waiting for transfers between devices  9.71 us (9%)
  Pallas kernels  7.73 us (7%)
  local copies, waits for them, and re-layouts  5.75 us (5%)
    all_to_all x4, blocking collectives, exchange(): return lax.all_to_all(array, axes, 0, 0, tiled=True)  63.6 us
    all_to_all x1, starting transfers between devices, exchange(): return lax.all_to_all(array, axes, 0, 0, tiled=True)  13 us
    ppermute x9, starting transfers between devices, shifted(): lax.ppermute(array, axis, [(i, (i + by) % count) for i in range(count)])  11.8 us
    pallas_call x8, Pallas kernels, call(): pl.pallas_call(kernel, name=name, out_shape=[jax.ShapeDtypeStruct(o, F32)...  7.73 us
    all_to_all x1, waiting for transfers between devices, exchange(): return lax.all_to_all(array, axes, 0, 0, tiled=True)  6.84 us
    unnamed x21, local copies, waits for them, and re-layouts  4.43 us
    ppermute x9, waiting for transfers between devices, shifted(): lax.ppermute(array, axis, [(i, (i + by) % count) for i in range(count)])  2.87 us
  transfers between devices with their start and end apart: 10, of which 5 were waited for; matrix products, arithmetic and copies ran while one was open for 0% of the time, Pallas kernels for 0%

profile of v2, /device:TPU:1, one launch (start us, length us, event | category | flops | bytes accessed | tf_op | source)
XLA Modules:
  0.0 112.3 jit_solution(15012348907866889319)
XLA Ops:
  0.6 0.0 copy-start.4
  0.6 0.0 copy-start.8
  0.7 0.7 copy-done.4
  1.3 0.0 copy-done.8
  1.3 0.0 copy-start
  1.3 0.9 copy-done
  2.2 0.7 copy-done.3
  3.0 0.7 copy-done.5
  3.7 0.7 copy-done.6
  4.3 0.7 copy-done.7
  5.0 1.0 pack.1
  6.0 0.9 copy.10
  6.9 13.0 %all-to-all-start = ((f32[64,1,768]{2,1,0:T(1,128)}), f32[64,1,768]{2,1,0:T(1,128)S(1)}, u32[]{:S(2)}, u32[]{:S(2)}) async-start(f32[64,1,768]{2,1,0:T(1,128)} %copy.10), calls=%async_computation | async-start | bytes 393216 | tf_op jit(solution)/shard_map/all_to_all | solution.py:389
  19.9 1.4 %collective-permute-start = (f32[3,16,128]{2,1,0:T(8,128)S(1)}, f32[3,16,128]{2,1,0:T(8,128)S(1)}, u32[]{:S(2)}, u32[]{:S(2)}) collective-permute-start(f32[3,16,128]{2,1,0:T(8,128)S(1)} %get-tuple-element.32), channel_id=1, source_target_pairs={{0,2},{2,4},{4,6},{6,8},{8,10},{10,12},{12,14},{14,16},{16,18},{18... | collective-permute-start | bytes 73736 | tf_op jit(solution)/shard_map/ppermute | solution.py:385
  21.3 3.7 %collective-permute-start.1 = (f32[3,16,128]{2,1,0:T(8,128)S(1)}, f32[3,16,128]{2,1,0:T(8,128)S(1)}, u32[]{:S(2)}, u32[]{:S(2)}) collective-permute-start(f32[3,16,128]{2,1,0:T(8,128)S(1)} %get-tuple-element.33), channel_id=1, source_target_pairs={{0,62},{2,0},{4,2},{6,4},{8,6},{10,8},{12,10},{14,12},{16,14},{18,... | collective-permute-start | bytes 73736 | tf_op jit(solution)/shard_map/ppermute | solution.py:385
  25.0 6.8 %all-to-all-done = f32[64,1,768]{2,1,0:T(1,128)S(1)} async-done(((f32[64,1,768]{2,1,0:T(1,128)}), f32[64,1,768]{2,1,0:T(1,128)S(1)}, u32[]{:S(2)}, u32[]{:S(2)}) %all-to-all-start) | async-done | bytes 196640 | tf_op jit(solution)/shard_map/all_to_all | solution.py:389
  31.9 0.0 collective-permute-done.refs_2_
  31.9 0.0 collective-permute-done.1.refs_3_
  31.9 0.0 copy-done.1
  31.9 0.0 copy-start.2
  31.9 0.8 spread0.1
  32.7 0.5 collective-permute-start.2
  33.2 1.3 %collective-permute-start.3 = (f32[3,8,128]{2,1,0:T(8,128)S(1)}, f32[3,8,128]{2,1,0:T(8,128)S(1)}, u32[]{:S(2)}, u32[]{:S(2)}) collective-permute-start(f32[3,8,128]{2,1,0:T(8,128)S(1)} %get-tuple-element.40), channel_id=1, source_target_pairs={{0,64},{64,128},{128,192},{192,0},{1,65},{65,129},{129,193},{193,1... | collective-permute-start | bytes 36872 | tf_op jit(solution)/shard_map/ppermute | solution.py:385
  34.5 1.4 %collective-permute-start.4 = (f32[3,8,128]{2,1,0:T(8,128)S(1)}, f32[3,8,128]{2,1,0:T(8,128)S(1)}, u32[]{:S(2)}, u32[]{:S(2)}) collective-permute-start(f32[3,8,128]{2,1,0:T(8,128)S(1)} %get-tuple-element.41), channel_id=1, source_target_pairs={{0,192},{64,0},{128,64},{192,128},{1,193},{65,1},{129,65},{193,129... | collective-permute-start | bytes 36872 | tf_op jit(solution)/shard_map/ppermute | solution.py:385
  35.9 1.1 collective-permute-done.3.refs_8_
  37.0 0.3 collective-permute-done.4.refs_9_
  37.3 0.0 collective-permute-done.2.refs_2_
  37.3 0.0 copy-done.2
  37.3 0.5 sample0.1
  37.8 0.2 copy.11
  38.0 18.3 %all_to_all.49 = f32[64,1,768]{2,1,0:T(1,128)S(1)} all-to-all(f32[64,1,768]{2,1,0:T(1,128)S(1)} %copy.11), channel_id=1, replica_groups=mesh['cable'=4,'fx'=32,'fz'=2] {'fx','fz'}, dimensions={0} | all-to-all | bytes 393216 | tf_op jit(solution)/shard_map/all_to_all | solution.py:389
  56.4 1.3 %spread1.1 = (f32[3,128,128]{2,1,0:T(8,128)S(1)}, f32[3,16,128]{2,1,0:T(8,128)S(1)}, f32[3,16,128]{2,1,0:T(8,128)S(1)}, f32[128,256]{1,0:T(8,128)S(1)}, f32[128,...) custom-call(f32[64,768]{1,0:T(8,128)S(1)} %bitcast.25, ...), custom_call_target="tpu_custom_call" | custom-call | bytes 1196032 | tf_op jit(solution)/shard_map/spread1/pallas_call | solution.py:371
  57.6 0.5 collective-permute-start.5
  58.1 1.3 %collective-permute-start.6 = (f32[3,8,128]{2,1,0:T(8,128)S(1)}, f32[3,8,128]{2,1,0:T(8,128)S(1)}, u32[]{:S(2)}, u32[]{:S(2)}) collective-permute-start(f32[3,8,128]{2,1,0:T(8,128)S(1)} %get-tuple-element.48), channel_id=1, source_target_pairs={{0,64},{64,128},{128,192},{192,0},{1,65},{65,129},{129,193},{193,1... | collective-permute-start | bytes 36872 | tf_op jit(solution)/shard_map/ppermute | solution.py:385
  59.4 1.4 %collective-permute-start.7 = (f32[3,8,128]{2,1,0:T(8,128)S(1)}, f32[3,8,128]{2,1,0:T(8,128)S(1)}, u32[]{:S(2)}, u32[]{:S(2)}) collective-permute-start(f32[3,8,128]{2,1,0:T(8,128)S(1)} %get-tuple-element.49), channel_id=1, source_target_pairs={{0,192},{64,0},{128,64},{192,128},{1,193},{65,1},{129,65},{193,129... | collective-permute-start | bytes 36872 | tf_op jit(solution)/shard_map/ppermute | solution.py:385
  60.8 1.1 collective-permute-done.6.refs_8_
  61.9 0.4 collective-permute-done.7.refs_9_
  62.2 0.0 collective-permute-done.5.refs_2_
  62.2 0.5 sample1.1
  62.8 0.2 copy.12
  63.0 17.6 %all_to_all.50 = f32[64,1,896]{2,1,0:T(1,128)S(1)} all-to-all(f32[64,1,896]{2,1,0:T(1,128)S(1)} %copy.12), channel_id=1, replica_groups=mesh['cable'=4,'fx'=32,'fz'=2] {'fx','fz'}, dimensions={0} | all-to-all | bytes 458752 | tf_op jit(solution)/shard_map/all_to_all | solution.py:389
  80.7 1.8 %spread2.1 = (f32[6,128,128]{2,1,0:T(8,128)S(1)}, f32[6,16,128]{2,1,0:T(8,128)S(1)}, f32[6,16,128]{2,1,0:T(8,128)S(1)}, f32[128,256]{1,0:T(8,128)S(1)}, f32[128,...) custom-call(f32[64,768]{1,0:T(8,128)S(1)} %bitcast.26, f32[3,128,128]{2,1,0:T(8,128)S(1)} %bitcast.23, ...), custom_call_target="tpu_custom_call" | custom-call | bytes 1761280 | tf_op jit(solution)/shard_map/spread2/pallas_call | solution.py:371
  82.5 0.3 collective-permute-start.8
  82.8 8.4 %all_to_all.51.refs_8_ = f32[4,7,8,128]{3,2,1,0:T(8,128)S(1)} all-to-all(f32[4,7,8,128]{3,2,1,0:T(8,128)S(1)} %get-tuple-element.56), channel_id=1, replica_groups=mesh['cable'=4,'fx'=32,'fz'=2] {'cable'}, dimensions={0} | all-to-all | bytes 229376 | tf_op jit(solution)/shard_map/all_to_all | solution.py:389
  91.2 0.0 collective-permute-done.8.refs_2_
  91.2 1.0 sample2.1
  92.2 19.3 %all_to_all.52 = f32[256,1,128]{2,1,0:T(1,128)S(1)} all-to-all(f32[256,1,128]{2,1,0:T(1,128)S(1)} %bitcast.37), channel_id=1, replica_groups=mesh['cable'=4,'fx'=32,'fz'=2] {'cable','fx','fz'}, dimensions={0} | all-to-all | bytes 262144 | tf_op jit(solution)/shard_map/all_to_all | solution.py:389
  111.5 0.8 finish.1
  (8 shorter events, 0.1 us)
Async XLA Ops:
  0.6 0.7 copy-start.4
  0.6 0.7 copy-start.8
  1.3 0.9 copy-start
  2.2 0.7 copy-start.3
  3.0 0.7 copy-start.5
  3.7 0.7 copy-start.6
  4.3 0.7 copy-start.7
  6.9 25.0 %all-to-all-start = ((f32[64,1,768]{2,1,0:T(1,128)}), f32[64,1,768]{2,1,0:T(1,128)S(1)}, u32[]{:S(2)}, u32[]{:S(2)}) async-start(f32[64,1,768]{2,1,0:T(1,128)} %copy.10), calls=%async_computation | async-start | bytes 393216 | tf_op jit(solution)/shard_map/all_to_all | solution.py:389
  19.9 12.0 %collective-permute-start = (f32[3,16,128]{2,1,0:T(8,128)S(1)}, f32[3,16,128]{2,1,0:T(8,128)S(1)}, u32[]{:S(2)}, u32[]{:S(2)}) collective-permute-start(f32[3,16,128]{2,1,0:T(8,128)S(1)} %get-tuple-element.32), channel_id=1, source_target_pairs={{0,2},{2,4},{4,6},{6,8},{8,10},{10,12},{12,14},{14,16},{16,18},{18... | collective-permute-start | bytes 73736 | tf_op jit(solution)/shard_map/ppermute | solution.py:385
  21.3 10.6 %copy-start.1 = (f32[3,8,16,128]{3,2,1,0:T(8,128)S(1)}, f32[3,8,16,128]{3,2,1,0:T(8,128)}, u32[]{:S(2)}) copy-start(f32[3,8,16,128]{3,2,1,0:T(8,128)} %param.8) | copy-start | bytes 589828
  21.3 10.6 %collective-permute-start.1 = (f32[3,16,128]{2,1,0:T(8,128)S(1)}, f32[3,16,128]{2,1,0:T(8,128)S(1)}, u32[]{:S(2)}, u32[]{:S(2)}) collective-permute-start(f32[3,16,128]{2,1,0:T(8,128)S(1)} %get-tuple-element.33), channel_id=1, source_target_pairs={{0,62},{2,0},{4,2},{6,4},{8,6},{10,8},{12,10},{14,12},{16,14},{18,... | collective-permute-start | bytes 73736 | tf_op jit(solution)/shard_map/ppermute | solution.py:385
  31.9 5.4 %copy-start.2 = (f32[8,16,128]{2,1,0:T(8,128)S(1)}, f32[8,16,128]{2,1,0:T(8,128)}, u32[]{:S(2)}) copy-start(f32[8,16,128]{2,1,0:T(8,128)} %param.9) | copy-start | bytes 196612
  32.7 4.6 %collective-permute-start.2 = (f32[3,128,128]{2,1,0:T(8,128)S(1)}, f32[3,128,128]{2,1,0:T(8,128)S(1)}, u32[]{:S(2)}, u32[]{:S(2)}) collective-permute-start(f32[3,128,128]{2,1,0:T(8,128)S(1)} %get-tuple-element.34.refs_1_), channel_id=1, source_target_pairs={{0,1},{1,0},{2,3},{3,2},{4,5},{5,4},{6,7},{7,6},{8,9},{9,8},{10,11... | collective-permute-start | bytes 589832 | tf_op jit(solution)/shard_map/ppermute | solution.py:385
  33.2 3.8 %collective-permute-start.3 = (f32[3,8,128]{2,1,0:T(8,128)S(1)}, f32[3,8,128]{2,1,0:T(8,128)S(1)}, u32[]{:S(2)}, u32[]{:S(2)}) collective-permute-start(f32[3,8,128]{2,1,0:T(8,128)S(1)} %get-tuple-element.40), channel_id=1, source_target_pairs={{0,64},{64,128},{128,192},{192,0},{1,65},{65,129},{129,193},{193,1... | collective-permute-start | bytes 36872 | tf_op jit(solution)/shard_map/ppermute | solution.py:385
  34.5 2.8 %collective-permute-start.4 = (f32[3,8,128]{2,1,0:T(8,128)S(1)}, f32[3,8,128]{2,1,0:T(8,128)S(1)}, u32[]{:S(2)}, u32[]{:S(2)}) collective-permute-start(f32[3,8,128]{2,1,0:T(8,128)S(1)} %get-tuple-element.41), channel_id=1, source_target_pairs={{0,192},{64,0},{128,64},{192,128},{1,193},{65,1},{129,65},{193,129... | collective-permute-start | bytes 36872 | tf_op jit(solution)/shard_map/ppermute | solution.py:385
  57.6 4.6 %collective-permute-start.5 = (f32[3,128,128]{2,1,0:T(8,128)S(1)}, f32[3,128,128]{2,1,0:T(8,128)S(1)}, u32[]{:S(2)}, u32[]{:S(2)}) collective-permute-start(f32[3,128,128]{2,1,0:T(8,128)S(1)} %get-tuple-element.42.refs_1_), channel_id=1, source_target_pairs={{0,1},{1,0},{2,3},{3,2},{4,5},{5,4},{6,7},{7,6},{8,9},{9,8},{10,11... | collective-permute-start | bytes 589832 | tf_op jit(solution)/shard_map/ppermute | solution.py:385
  58.1 3.8 %collective-permute-start.6 = (f32[3,8,128]{2,1,0:T(8,128)S(1)}, f32[3,8,128]{2,1,0:T(8,128)S(1)}, u32[]{:S(2)}, u32[]{:S(2)}) collective-permute-start(f32[3,8,128]{2,1,0:T(8,128)S(1)} %get-tuple-element.48), channel_id=1, source_target_pairs={{0,64},{64,128},{128,192},{192,0},{1,65},{65,129},{129,193},{193,1... | collective-permute-start | bytes 36872 | tf_op jit(solution)/shard_map/ppermute | solution.py:385
  59.4 2.8 %collective-permute-start.7 = (f32[3,8,128]{2,1,0:T(8,128)S(1)}, f32[3,8,128]{2,1,0:T(8,128)S(1)}, u32[]{:S(2)}, u32[]{:S(2)}) collective-permute-start(f32[3,8,128]{2,1,0:T(8,128)S(1)} %get-tuple-element.49), channel_id=1, source_target_pairs={{0,192},{64,0},{128,64},{192,128},{1,193},{65,1},{129,65},{193,129... | collective-permute-start | bytes 36872 | tf_op jit(solution)/shard_map/ppermute | solution.py:385
  82.5 8.7 %collective-permute-start.8 = (f32[6,128,128]{2,1,0:T(8,128)S(1)}, f32[6,128,128]{2,1,0:T(8,128)S(1)}, u32[]{:S(2)}, u32[]{:S(2)}) collective-permute-start(f32[6,128,128]{2,1,0:T(8,128)S(1)} %get-tuple-element.50.refs_1_), channel_id=1, source_target_pairs={{0,1},{1,0},{2,3},{3,2},{4,5},{5,4},{6,7},{7,6},{8,9},{9,8},{10,11... | collective-permute-start | bytes 1179656 | tf_op jit(solution)/shard_map/ppermute | solution.py:385

commit v3 on v2

--- a/solution.py
+++ b/solution.py
@@ -397,7 +397,7 @@
     msg, place, xlo, xhi = call(
         pack_kernel,
         "pack",
-        (*ins, flow),
+        tuple(pltpu.with_memory_space_constraint(a, pltpu.HBM) for a in (*ins, flow)),
         [(GROUP, FIELDS), (8, SEG_DEV), (3, SY, SZ), (3, SY, SZ)],
         [pltpu.VMEM(a.shape, a.dtype) for a in ins]
         + [pltpu.VMEM((24, SEG_DEV), F32), pltpu.VMEM((FIELDS, 128), F32), pltpu.SemaphoreType.DMA((8,))],

time: 113 us -> 109 us (0.965)
  local copies, waits for them, and re-layouts: 5.75 us -> 1.37 us
    unnamed x21 -> x7, local copies, waits for them, and re-layouts: 4.43 us -> 0.05 us
where the time goes in v3:
time: 109 us
  blocking collectives  63.6 us (58%)
  starting transfers between devices  24.8 us (23%)
  waiting for transfers between devices  9.71 us (9%)
  Pallas kernels  8.52 us (8%)
  local copies, waits for them, and re-layouts  1.37 us (1%)
    all_to_all x4, blocking collectives, exchange(): return lax.all_to_all(array, axes, 0, 0, tiled=True)  63.6 us
    all_to_all x1, starting transfers between devices, exchange(): return lax.all_to_all(array, axes, 0, 0, tiled=True)  13 us
    ppermute x9, starting transfers between devices, shifted(): lax.ppermute(array, axis, [(i, (i + by) % count) for i in range(count)])  11.8 us
    pallas_call x8, Pallas kernels, call(): pl.pallas_call(kernel, name=name, out_shape=[jax.ShapeDtypeStruct(o, F32)...  8.52 us
    all_to_all x1, waiting for transfers between devices, exchange(): return lax.all_to_all(array, axes, 0, 0, tiled=True)  6.84 us
    ppermute x9, waiting for transfers between devices, shifted(): lax.ppermute(array, axis, [(i, (i + by) % count) for i in range(count)])  2.87 us
  transfers between devices with their start and end apart: 10, of which 5 were waited for; matrix products, arithmetic and copies ran while one was open for 0% of the time, Pallas kernels for 0%

profile of v3, /device:TPU:1, one launch (start us, length us, event | category | flops | bytes accessed | tf_op | source)
XLA Modules:
  0.0 108.7 jit_solution(2796516234667144655)
XLA Ops:
  0.6 1.7 %pack.1 = (f32[64,768]{1,0:T(8,128)S(1)}, f32[8,64]{1,0:T(8,128)S(1)}, f32[3,16,128]{2,1,0:T(8,128)S(1)}, f32[3,16,128]{2,1,0:T(8,128)S(1)}) custom-call(f32[3,64]{1,0:T(4,128)} %refs_0_.1, f32[3,64]{1,0:T(4,128)} %refs_1_.1, f32[1,64]{1,0:T(1,128)} %bitcast.38, f32[3,12,64]{2,1,0:T(8,128)} %refs_3_.1, s32[3,64]{1,0:T(4,128)} %refs_4_.1, s32[3,64]{1,0:T(4,128)} %refs_5_.1, ...), custom_call_target="tpu_custom_call" | custom-call | bytes 456960 | tf_op jit(solution)/shard_map/pack/pallas_call | solution.py:371
  2.4 0.9 copy.10
  3.3 13.0 %all-to-all-start = ((f32[64,1,768]{2,1,0:T(1,128)}), f32[64,1,768]{2,1,0:T(1,128)S(1)}, u32[]{:S(2)}, u32[]{:S(2)}) async-start(f32[64,1,768]{2,1,0:T(1,128)} %copy.10), calls=%async_computation | async-start | bytes 393216 | tf_op jit(solution)/shard_map/all_to_all | solution.py:389
  16.2 1.4 %collective-permute-start = (f32[3,16,128]{2,1,0:T(8,128)S(1)}, f32[3,16,128]{2,1,0:T(8,128)S(1)}, u32[]{:S(2)}, u32[]{:S(2)}) collective-permute-start(f32[3,16,128]{2,1,0:T(8,128)S(1)} %get-tuple-element.32), channel_id=1, source_target_pairs={{0,2},{2,4},{4,6},{6,8},{8,10},{10,12},{12,14},{14,16},{16,18},{18... | collective-permute-start | bytes 73736 | tf_op jit(solution)/shard_map/ppermute | solution.py:385
  17.7 0.0 copy-start
  17.7 3.7 %collective-permute-start.1 = (f32[3,16,128]{2,1,0:T(8,128)S(1)}, f32[3,16,128]{2,1,0:T(8,128)S(1)}, u32[]{:S(2)}, u32[]{:S(2)}) collective-permute-start(f32[3,16,128]{2,1,0:T(8,128)S(1)} %get-tuple-element.33), channel_id=1, source_target_pairs={{0,62},{2,0},{4,2},{6,4},{8,6},{10,8},{12,10},{14,12},{16,14},{18,... | collective-permute-start | bytes 73736 | tf_op jit(solution)/shard_map/ppermute | solution.py:385
  21.4 6.8 %all-to-all-done = f32[64,1,768]{2,1,0:T(1,128)S(1)} async-done(((f32[64,1,768]{2,1,0:T(1,128)}), f32[64,1,768]{2,1,0:T(1,128)S(1)}, u32[]{:S(2)}, u32[]{:S(2)}) %all-to-all-start) | async-done | bytes 196640 | tf_op jit(solution)/shard_map/all_to_all | solution.py:389
  28.3 0.0 collective-permute-done.refs_2_
  28.3 0.0 collective-permute-done.1.refs_3_
  28.3 0.0 copy-done
  28.3 0.0 copy-start.1
  28.3 0.8 spread0.1
  29.1 0.5 collective-permute-start.2
  29.6 1.3 %collective-permute-start.3 = (f32[3,8,128]{2,1,0:T(8,128)S(1)}, f32[3,8,128]{2,1,0:T(8,128)S(1)}, u32[]{:S(2)}, u32[]{:S(2)}) collective-permute-start(f32[3,8,128]{2,1,0:T(8,128)S(1)} %get-tuple-element.40), channel_id=1, source_target_pairs={{0,64},{64,128},{128,192},{192,0},{1,65},{65,129},{129,193},{193,1... | collective-permute-start | bytes 36872 | tf_op jit(solution)/shard_map/ppermute | solution.py:385
  30.9 1.4 %collective-permute-start.4 = (f32[3,8,128]{2,1,0:T(8,128)S(1)}, f32[3,8,128]{2,1,0:T(8,128)S(1)}, u32[]{:S(2)}, u32[]{:S(2)}) collective-permute-start(f32[3,8,128]{2,1,0:T(8,128)S(1)} %get-tuple-element.41), channel_id=1, source_target_pairs={{0,192},{64,0},{128,64},{192,128},{1,193},{65,1},{129,65},{193,129... | collective-permute-start | bytes 36872 | tf_op jit(solution)/shard_map/ppermute | solution.py:385
  32.3 1.1 collective-permute-done.3.refs_8_
  33.4 0.3 collective-permute-done.4.refs_9_
  33.7 0.0 collective-permute-done.2.refs_2_
  33.7 0.0 copy-done.1
  33.7 0.5 sample0.1
  34.2 0.2 copy.11
  34.4 18.3 %all_to_all.49 = f32[64,1,768]{2,1,0:T(1,128)S(1)} all-to-all(f32[64,1,768]{2,1,0:T(1,128)S(1)} %copy.11), channel_id=1, replica_groups=mesh['cable'=4,'fx'=32,'fz'=2] {'fx','fz'}, dimensions={0} | all-to-all | bytes 393216 | tf_op jit(solution)/shard_map/all_to_all | solution.py:389
  52.7 1.3 %spread1.1 = (f32[3,128,128]{2,1,0:T(8,128)S(1)}, f32[3,16,128]{2,1,0:T(8,128)S(1)}, f32[3,16,128]{2,1,0:T(8,128)S(1)}, f32[128,256]{1,0:T(8,128)S(1)}, f32[128,...) custom-call(f32[64,768]{1,0:T(8,128)S(1)} %bitcast.25, ...), custom_call_target="tpu_custom_call" | custom-call | bytes 1196032 | tf_op jit(solution)/shard_map/spread1/pallas_call | solution.py:371
  54.0 0.5 collective-permute-start.5
  54.5 1.3 %collective-permute-start.6 = (f32[3,8,128]{2,1,0:T(8,128)S(1)}, f32[3,8,128]{2,1,0:T(8,128)S(1)}, u32[]{:S(2)}, u32[]{:S(2)}) collective-permute-start(f32[3,8,128]{2,1,0:T(8,128)S(1)} %get-tuple-element.48), channel_id=1, source_target_pairs={{0,64},{64,128},{128,192},{192,0},{1,65},{65,129},{129,193},{193,1... | collective-permute-start | bytes 36872 | tf_op jit(solution)/shard_map/ppermute | solution.py:385
  55.8 1.4 %collective-permute-start.7 = (f32[3,8,128]{2,1,0:T(8,128)S(1)}, f32[3,8,128]{2,1,0:T(8,128)S(1)}, u32[]{:S(2)}, u32[]{:S(2)}) collective-permute-start(f32[3,8,128]{2,1,0:T(8,128)S(1)} %get-tuple-element.49), channel_id=1, source_target_pairs={{0,192},{64,0},{128,64},{192,128},{1,193},{65,1},{129,65},{193,129... | collective-permute-start | bytes 36872 | tf_op jit(solution)/shard_map/ppermute | solution.py:385
  57.2 1.1 collective-permute-done.6.refs_8_
  58.2 0.4 collective-permute-done.7.refs_9_
  58.6 0.0 collective-permute-done.5.refs_2_
  58.6 0.5 sample1.1
  59.2 0.2 copy.12
  59.4 17.6 %all_to_all.50 = f32[64,1,896]{2,1,0:T(1,128)S(1)} all-to-all(f32[64,1,896]{2,1,0:T(1,128)S(1)} %copy.12), channel_id=1, replica_groups=mesh['cable'=4,'fx'=32,'fz'=2] {'fx','fz'}, dimensions={0} | all-to-all | bytes 458752 | tf_op jit(solution)/shard_map/all_to_all | solution.py:389
  77.0 1.8 %spread2.1 = (f32[6,128,128]{2,1,0:T(8,128)S(1)}, f32[6,16,128]{2,1,0:T(8,128)S(1)}, f32[6,16,128]{2,1,0:T(8,128)S(1)}, f32[128,256]{1,0:T(8,128)S(1)}, f32[128,...) custom-call(f32[64,768]{1,0:T(8,128)S(1)} %bitcast.26, f32[3,128,128]{2,1,0:T(8,128)S(1)} %bitcast.23, ...), custom_call_target="tpu_custom_call" | custom-call | bytes 1761280 | tf_op jit(solution)/shard_map/spread2/pallas_call | solution.py:371
  78.9 0.3 collective-permute-start.8
  79.2 8.4 %all_to_all.51.refs_8_ = f32[4,7,8,128]{3,2,1,0:T(8,128)S(1)} all-to-all(f32[4,7,8,128]{3,2,1,0:T(8,128)S(1)} %get-tuple-element.56), channel_id=1, replica_groups=mesh['cable'=4,'fx'=32,'fz'=2] {'cable'}, dimensions={0} | all-to-all | bytes 229376 | tf_op jit(solution)/shard_map/all_to_all | solution.py:389
  87.6 0.0 collective-permute-done.8.refs_2_
  87.6 1.0 sample2.1
  88.6 19.3 %all_to_all.52 = f32[256,1,128]{2,1,0:T(1,128)S(1)} all-to-all(f32[256,1,128]{2,1,0:T(1,128)S(1)} %bitcast.37), channel_id=1, replica_groups=mesh['cable'=4,'fx'=32,'fz'=2] {'cable','fx','fz'}, dimensions={0} | all-to-all | bytes 262144 | tf_op jit(solution)/shard_map/all_to_all | solution.py:389
  107.9 0.8 finish.1
  (3 shorter events, 0.0 us)
Async XLA Ops:
  3.3 25.0 %all-to-all-start = ((f32[64,1,768]{2,1,0:T(1,128)}), f32[64,1,768]{2,1,0:T(1,128)S(1)}, u32[]{:S(2)}, u32[]{:S(2)}) async-start(f32[64,1,768]{2,1,0:T(1,128)} %copy.10), calls=%async_computation | async-start | bytes 393216 | tf_op jit(solution)/shard_map/all_to_all | solution.py:389
  16.2 12.0 %collective-permute-start = (f32[3,16,128]{2,1,0:T(8,128)S(1)}, f32[3,16,128]{2,1,0:T(8,128)S(1)}, u32[]{:S(2)}, u32[]{:S(2)}) collective-permute-start(f32[3,16,128]{2,1,0:T(8,128)S(1)} %get-tuple-element.32), channel_id=1, source_target_pairs={{0,2},{2,4},{4,6},{6,8},{8,10},{10,12},{12,14},{14,16},{16,18},{18... | collective-permute-start | bytes 73736 | tf_op jit(solution)/shard_map/ppermute | solution.py:385
  17.7 10.6 %copy-start = (f32[3,8,16,128]{3,2,1,0:T(8,128)S(1)}, f32[3,8,16,128]{3,2,1,0:T(8,128)}, u32[]{:S(2)}) copy-start(f32[3,8,16,128]{3,2,1,0:T(8,128)} %param.8) | copy-start | bytes 589828
  17.7 10.6 %collective-permute-start.1 = (f32[3,16,128]{2,1,0:T(8,128)S(1)}, f32[3,16,128]{2,1,0:T(8,128)S(1)}, u32[]{:S(2)}, u32[]{:S(2)}) collective-permute-start(f32[3,16,128]{2,1,0:T(8,128)S(1)} %get-tuple-element.33), channel_id=1, source_target_pairs={{0,62},{2,0},{4,2},{6,4},{8,6},{10,8},{12,10},{14,12},{16,14},{18,... | collective-permute-start | bytes 73736 | tf_op jit(solution)/shard_map/ppermute | solution.py:385
  28.3 5.4 %copy-start.1 = (f32[8,16,128]{2,1,0:T(8,128)S(1)}, f32[8,16,128]{2,1,0:T(8,128)}, u32[]{:S(2)}) copy-start(f32[8,16,128]{2,1,0:T(8,128)} %param.9) | copy-start | bytes 196612
  29.1 4.6 %collective-permute-start.2 = (f32[3,128,128]{2,1,0:T(8,128)S(1)}, f32[3,128,128]{2,1,0:T(8,128)S(1)}, u32[]{:S(2)}, u32[]{:S(2)}) collective-permute-start(f32[3,128,128]{2,1,0:T(8,128)S(1)} %get-tuple-element.34.refs_1_), channel_id=1, source_target_pairs={{0,1},{1,0},{2,3},{3,2},{4,5},{5,4},{6,7},{7,6},{8,9},{9,8},{10,11... | collective-permute-start | bytes 589832 | tf_op jit(solution)/shard_map/ppermute | solution.py:385
  29.6 3.8 %collective-permute-start.3 = (f32[3,8,128]{2,1,0:T(8,128)S(1)}, f32[3,8,128]{2,1,0:T(8,128)S(1)}, u32[]{:S(2)}, u32[]{:S(2)}) collective-permute-start(f32[3,8,128]{2,1,0:T(8,128)S(1)} %get-tuple-element.40), channel_id=1, source_target_pairs={{0,64},{64,128},{128,192},{192,0},{1,65},{65,129},{129,193},{193,1... | collective-permute-start | bytes 36872 | tf_op jit(solution)/shard_map/ppermute | solution.py:385
  30.9 2.8 %collective-permute-start.4 = (f32[3,8,128]{2,1,0:T(8,128)S(1)}, f32[3,8,128]{2,1,0:T(8,128)S(1)}, u32[]{:S(2)}, u32[]{:S(2)}) collective-permute-start(f32[3,8,128]{2,1,0:T(8,128)S(1)} %get-tuple-element.41), channel_id=1, source_target_pairs={{0,192},{64,0},{128,64},{192,128},{1,193},{65,1},{129,65},{193,129... | collective-permute-start | bytes 36872 | tf_op jit(solution)/shard_map/ppermute | solution.py:385
  54.0 4.6 %collective-permute-start.5 = (f32[3,128,128]{2,1,0:T(8,128)S(1)}, f32[3,128,128]{2,1,0:T(8,128)S(1)}, u32[]{:S(2)}, u32[]{:S(2)}) collective-permute-start(f32[3,128,128]{2,1,0:T(8,128)S(1)} %get-tuple-element.42.refs_1_), channel_id=1, source_target_pairs={{0,1},{1,0},{2,3},{3,2},{4,5},{5,4},{6,7},{7,6},{8,9},{9,8},{10,11... | collective-permute-start | bytes 589832 | tf_op jit(solution)/shard_map/ppermute | solution.py:385
  54.5 3.8 %collective-permute-start.6 = (f32[3,8,128]{2,1,0:T(8,128)S(1)}, f32[3,8,128]{2,1,0:T(8,128)S(1)}, u32[]{:S(2)}, u32[]{:S(2)}) collective-permute-start(f32[3,8,128]{2,1,0:T(8,128)S(1)} %get-tuple-element.48), channel_id=1, source_target_pairs={{0,64},{64,128},{128,192},{192,0},{1,65},{65,129},{129,193},{193,1... | collective-permute-start | bytes 36872 | tf_op jit(solution)/shard_map/ppermute | solution.py:385
  55.8 2.8 %collective-permute-start.7 = (f32[3,8,128]{2,1,0:T(8,128)S(1)}, f32[3,8,128]{2,1,0:T(8,128)S(1)}, u32[]{:S(2)}, u32[]{:S(2)}) collective-permute-start(f32[3,8,128]{2,1,0:T(8,128)S(1)} %get-tuple-element.49), channel_id=1, source_target_pairs={{0,192},{64,0},{128,64},{192,128},{1,193},{65,1},{129,65},{193,129... | collective-permute-start | bytes 36872 | tf_op jit(solution)/shard_map/ppermute | solution.py:385
  78.9 8.7 %collective-permute-start.8 = (f32[6,128,128]{2,1,0:T(8,128)S(1)}, f32[6,128,128]{2,1,0:T(8,128)S(1)}, u32[]{:S(2)}, u32[]{:S(2)}) collective-permute-start(f32[6,128,128]{2,1,0:T(8,128)S(1)} %get-tuple-element.50.refs_1_), channel_id=1, source_target_pairs={{0,1},{1,0},{2,3},{3,2},{4,5},{5,4},{6,7},{7,6},{8,9},{9,8},{10,11... | collective-permute-start | bytes 1179656 | tf_op jit(solution)/shard_map/ppermute | solution.py:385
